TPU v7x, 512 devices: a whole 4x8x8 slice. The times are simulated.
512 devices in a mesh: video: 16 (over x, z_hi, core), tm: 32 (over y, z_lo).
Axes of the slice: x: 4, y: 8, z: 8 (z_hi: 2, z_lo: 4; z = z_hi * 4 + z_lo), core: 2. Of those that a mesh axis runs over, the one named last changes fastest.
Arguments:
- frames: bfloat16 [512, 28, 28, 704], P(('video', 'tm')), parts along dimension 0, may hold values from -6 to 6
- clip_cut: int32 [512], P(('video', 'tm')), parts along dimension 0, may hold values 0 or 1
- space_kernel: float32 [49, 704], replicated, may hold values from -0.8 to 0.8
- time_kernel: float32 [3, 704], replicated, may hold values from -3 to 3
- conv_bias: float32 [704], replicated, may hold values from -3 to 3
- norm_gain: float32 [704], replicated, may hold values from 0.5 to 1.5
- norm_bias: float32 [704], replicated, may hold values from -3 to 3
- up_weight: bfloat16 [704, 2816], P(None, 'tm'), may hold values from -0.21875 to 0.21875
- up_bias: float32 [2816], replicated, may hold values from -3 to 3
- grn_gamma: float32 [2816], replicated, may hold values from -3 to 3
- grn_beta: float32 [2816], replicated, may hold values from -3 to 3
- down_weight: bfloat16 [2816, 704], P('tm'), may hold values from -0.109375 to 0.109375
- down_bias: float32 [704], replicated, may hold values from -3 to 3
Outputs:
- block_out: bfloat16 [512, 28, 28, 704], P(('video', 'tm')), parts along dimension 0
There are 16 independent parts, one for each index of `video`. A program takes and returns all parts, laid end to end along the dimension named above; an argument that names none is the same for every part. Nothing has to cross between parts.
All inputs are finite; a program needn't handle non-finite values. No bound on the sum of `clip_cut` on one device may be relied on, other than what follows from the above.
Results may differ from a plain program's by a relative error of at most 0.0054.
Values may be sent and summed in bfloat16 or wider, within the bound.
No kernel may reach another device: no remote copies, remote signals or barrier semaphores. Data moves between devices by JAX's collectives and lax.ppermute only.
A program may use at most 64 MiB of HBM per device.

v0:
```python
import jax
import jax.numpy as jnp
from jax import lax
from jax.sharding import PartitionSpec as P


def from_behind(value, axis, by):
    count = lax.axis_size(axis)
    pairs = [(i, i + by) for i in range(count) if 0 <= i + by < count]
    return lax.ppermute(value, axis, pairs)


def space_time(frames, prev_side, next_side, space_kernel, time_kernel, conv_bias):
    padded = jnp.pad(frames, ((0, 0), (3, 3), (3, 3), (0, 0)))
    total = jnp.zeros(frames.shape, jnp.float32)
    for row_off in range(7):
        for col_off in range(7):
            window = padded[
                :, row_off : row_off + frames.shape[1], col_off : col_off + frames.shape[2], :
            ]
            total = total + window.astype(jnp.float32) * space_kernel[7 * row_off + col_off]
    total = total + time_kernel[0] * prev_side.astype(jnp.float32)
    total = total + time_kernel[1] * frames.astype(jnp.float32)
    total = total + time_kernel[2] * next_side.astype(jnp.float32)
    return total + conv_bias


def layer_norm(conv, norm_gain, norm_bias):
    mean_val = jnp.mean(conv, axis=-1, keepdims=True)
    centered = conv - mean_val
    var_val = jnp.mean(centered * centered, axis=-1, keepdims=True)
    return (centered / jnp.sqrt(var_val + 1e-06) * norm_gain + norm_bias).astype(jnp.bfloat16)


def response_norm(hidden, grn_gamma, grn_beta, frame_count):
    hid32 = hidden.astype(jnp.float32).reshape(frame_count, -1, hidden.shape[-1])
    energy = jnp.sqrt(jnp.sum(hid32 * hid32, axis=1, keepdims=True))
    ratio = energy / (jnp.mean(energy, axis=2, keepdims=True) + 1e-06)
    result = grn_gamma * hid32 * ratio + grn_beta + hid32
    return result.reshape(hidden.shape).astype(jnp.bfloat16)


def per_device(
    frames,
    clip_cut,
    space_kernel,
    time_kernel,
    conv_bias,
    norm_gain,
    norm_bias,
    up_weight,
    up_bias,
    grn_gamma,
    grn_beta,
    down_weight,
    down_bias,
):
    frame_count = frames.shape[0]
    keep = (1 - clip_cut).astype(jnp.bfloat16)[:, None, None, None]
    masked = frames * keep
    from_before = from_behind(frames, "tm", 1)
    from_after = from_behind(masked, "tm", -1)
    prev_side = jnp.concatenate([from_before, frames[:-1]], axis=0) * keep
    next_side = jnp.concatenate([masked[1:], from_after], axis=0)
    conv = space_time(frames, prev_side, next_side, space_kernel, time_kernel, conv_bias)
    rows = conv.reshape(-1, conv.shape[-1])
    normed = layer_norm(rows, norm_gain, norm_bias)
    residual = frames.reshape(rows.shape).astype(jnp.float32)
    hidden = jax.nn.gelu(
        jnp.dot(
            normed,
            lax.all_gather(up_weight, "tm", axis=1, tiled=True),
            preferred_element_type=jnp.float32,
        )
        + up_bias,
        approximate=False,
    ).astype(jnp.bfloat16)
    grn = response_norm(hidden, grn_gamma, grn_beta, frame_count)
    whole_down = lax.all_gather(down_weight, "tm", axis=0, tiled=True)
    projected = jnp.dot(grn, whole_down, preferred_element_type=jnp.float32)
    result = projected + down_bias + residual
    return result.astype(jnp.bfloat16).reshape(frames.shape)


def solution(mesh):
    return jax.shard_map(
        per_device,
        mesh=mesh,
        in_specs=(
            P(("video", "tm"), None, None, None),
            P(("video", "tm")),
            P(),
            P(),
            P(),
            P(),
            P(),
            P(None, "tm"),
            P(),
            P(),
            P(),
            P("tm", None),
            P(),
        ),
        out_specs=P(("video", "tm"), None, None, None),
        check_vma=False,
    )
```

profile of v0, /device:TPU:2, one launch (start us, length us, event | category | flops | bytes accessed | tf_op | source)
XLA Modules:
  0.0 385.6 jit_solution(17446686696309131363)
XLA Ops:
  6.5 0.0 copy-start
  6.5 0.0 all-gather.3.cloned.1.call-start
  6.5 0.7 all-gather.3.cloned.1.call-update
  7.3 0.0 all-gather.5.cloned.1.call-start
  8.0 0.0 copy-start.3
  8.0 0.0 copy-start.4
  8.0 2.5 broadcast_multiply_fusion
  10.5 0.0 copy-start.5
  10.5 1.4 collective-permute-start.1
  11.9 0.0 copy-done
  12.0 6.0 %collective-permute-start = (bf16[1,28,28,704]{3,2,1,0:T(8,128)(2,1)S(1)}, bf16[1,28,28,704]{3,2,1,0:T(8,128)(2,1)}, u32[]{:S(2)}, u32[]{:S(2)}) collective-permute-start(bf16[1,28,28,704]{3,2,1,0:T(8,128)(2,1)S(1)} %copy-done), channel_id=1, source_target_pairs={{0,1},{1,2},{2,3},{3,4},{4,5},{5,6},{6,7},{7,8},{8,9},{9,10},{10,1... | collective-permute-start | bytes 3311624 | tf_op jit(solution)/shard_map/ppermute | solution.py:10
  17.9 0.0 all-gather.5.cloned.1.call-update
  18.0 1.6 reshape.250
  19.6 0.0 copy-done.3
  19.6 0.0 copy-done.4
  19.6 0.1 slice_reduce_fusion.2
  19.7 0.2 slice_reduce_fusion.50
  19.9 0.2 slice_reduce_fusion.51
  20.1 29.9 %collective-permute-done.1 = bf16[1,28,28,704]{3,2,1,0:T(8,128)(2,1)S(1)} collective-permute-done((bf16[1,28,28,704]{3,2,1,0:T(8,128)(2,1)}, bf16[1,28,28,704]{3,2,1,0:T(8,128)(2,1)S(1)}, u32[]{:S(2)}, u32[]{:S(2)}) %collective-permute-start.1) | collective-permute-done | bytes 1103904 | tf_op jit(solution)/shard_map/ppermute | solution.py:10
  50.0 0.0 copy-start.2
  50.0 68.8 %collective-permute-done = bf16[1,28,28,704]{3,2,1,0:T(8,128)(2,1)} collective-permute-done((bf16[1,28,28,704]{3,2,1,0:T(8,128)(2,1)S(1)}, bf16[1,28,28,704]{3,2,1,0:T(8,128)(2,1)}, u32[]{:S(2)}, u32[]{:S(2)}) %collective-permute-start) | collective-permute-done | bytes 1103904 | tf_op jit(solution)/shard_map/ppermute | solution.py:10
  118.8 0.0 copy-done.2
  118.8 0.0 copy-done.5
  118.8 53.5 %fusion.25 = (f32[28,28]{1,0:T(8,128)S(1)}, f32[1,28,28,704]{3,2,1,0:T(8,128)S(1)}) fusion(f32[704]{0:T(1024)S(1)} %copy-done.5, bf16[1,28,28,704]{3,2,1,0:T(8,128)(2,1)} %copy-done.2, f32[704]{0:T(1024)S(1)} %get-tuple-element.55, f32[704]{0:T(1024)S(1)} %get-tuple-element.56, bf16[1,28,28,704]{3,2,1,0:T(8,128)(2,1)} %collective-permute-done, bf16[]{:T(256)} %bitcast, ...), kind=kLoop, calls=%fused_computation.143 | loop fusion | flops 87757040 | bytes 5671746 | tf_op jit(solution)/shard_map/reduce_sum | solution.py:29
  172.3 0.0 copy-start.6
  172.3 0.0 copy-start.9
  172.3 0.0 copy-start.10
  172.3 1.5 reshape.248
  173.9 0.1 div.33
  174.0 0.4 multiply_reduce_fusion
  174.4 0.1 sqrt.25
  174.5 0.0 copy-start.1
  174.5 0.0 copy-start.7
  174.5 0.0 copy-start.8
  174.6 0.0 copy-start.11
  174.6 25.7 %all-gather.3.cloned.1.call-done = bf16[704,2816]{0,1:T(8,128)(2,1)} async-done(((bf16[704,88]{0,1:T(8,128)(2,1)}), bf16[704,2816]{0,1:T(8,128)(2,1)}) %all-gather.3.cloned.1.call-update) | async-done | bytes 3964944 | tf_op jit(solution)/shard_map/all_gather | solution.py:72
  200.3 0.0 copy-done.6
  200.3 0.0 copy-done.9
  200.3 0.0 copy-done.10
  200.3 26.3 %fusion.5 = (f32[2816]{0:T(1024)S(1)}, bf16[784,2816]{1,0:T(8,128)(2,1)}) fusion(f32[2816]{0:T(1024)S(1)} %copy-done.6, bf16[704,2816]{0,1:T(8,128)(2,1)} %all-gather.3.cloned.1.call-done, f32[784,704]{1,0:T(8,128)} %reshape.248, f32[704]{0:T(1024)S(1)} %copy-done.9, f32[704]{0:T(1024)S(1)} %copy-done.10, f32[784]{0:T(1024)S(1)} %sqrt.25, f32[784]{0:T(1024)S(1)} %div.33), kind=kOutput, calls=%fused_computation.9 | convolution fusion | flops 3263594752 | bytes 10622592 | tf_op jit(solution)/shard_map/dot_general | solution.py:70
  226.6 0.6 sqrt_reduce_fusion
  227.9 139.0 %all-gather.5.cloned.1.call-done = bf16[2816,704]{1,0:T(8,128)(2,1)} async-done(((bf16[88,704]{1,0:T(8,128)(2,1)}), bf16[2816,704]{1,0:T(8,128)(2,1)}) %all-gather.5.cloned.1.call-update) | async-done | bytes 3964944 | tf_op jit(solution)/shard_map/all_gather | solution.py:79
  366.8 0.0 copy-done.1
  366.8 0.0 copy-done.7
  366.8 0.0 copy-done.8
  366.8 0.0 copy-done.11
  366.8 8.8 %add_convert_fusion = bf16[784,704]{1,0:T(8,128)(2,1)} fusion(f32[784,704]{1,0:T(8,128)S(1)} %copy-done.1, bf16[2816,704]{1,0:T(8,128)(2,1)} %all-gather.5.cloned.1.call-done, bf16[784,2816]{1,0:T(8,128)(2,1)} %get-tuple-element.60, f32[2816]{0:T(1024)S(1)} %copy-done.7, f32[2816]{0:T(1024)S(1)} %sqrt_divide_fusion, f32[2816]{0:T(1024)S(1)} %copy-done.8, ...), kind=kOutput, calls=%fused_computation.80 | convolution fusion | flops 3123405824 | bytes 11728640 | tf_op jit(solution)/shard_map/dot_general | solution.py:80
  375.6 3.2 reshape.249
  (3 shorter events, 0.0 us)
Async XLA Ops:
  6.5 5.4 %copy-start = (bf16[1,28,28,704]{3,2,1,0:T(8,128)(2,1)S(1)}, bf16[1,28,28,704]{3,2,1,0:T(8,128)(2,1)}, u32[]{:S(2)}) copy-start(bf16[1,28,28,704]{3,2,1,0:T(8,128)(2,1)} %param.13) | copy-start | bytes 3311620
  6.5 193.8 %all-gather.3.cloned.1.call-start = ((), (), s32[]{:S(2)}) async-start(), calls=%async_computation | async-start | bytes 4460544 | tf_op jit(solution)/shard_map/all_gather | solution.py:72
  7.3 359.6 %all-gather.5.cloned.1.call-start = ((), (), s32[]{:S(2)}) async-start(), calls=%async_computation.1 | async-start | bytes 4460544 | tf_op jit(solution)/shard_map/all_gather | solution.py:79
  8.0 11.6 %copy-start.3 = (f32[49,704]{1,0:T(8,128)S(1)}, f32[49,704]{1,0:T(8,128)}, u32[]{:S(2)}) copy-start(f32[49,704]{1,0:T(8,128)} %param.15) | copy-start | bytes 413956
  8.0 11.6 %copy-start.4 = (f32[3,704]{1,0:T(4,128)S(1)}, f32[3,704]{1,0:T(4,128)}, u32[]{:S(2)}) copy-start(f32[3,704]{1,0:T(4,128)} %param.16) | copy-start | bytes 25348
  10.5 108.3 %copy-start.5 = (f32[704]{0:T(1024)S(1)}, f32[704]{0:T(1024)}, u32[]{:S(2)}) copy-start(f32[704]{0:T(1024)} %param.17) | copy-start | bytes 8452
  10.5 39.5 %collective-permute-start.1 = (bf16[1,28,28,704]{3,2,1,0:T(8,128)(2,1)}, bf16[1,28,28,704]{3,2,1,0:T(8,128)(2,1)S(1)}, u32[]{:S(2)}, u32[]{:S(2)}) collective-permute-start(bf16[1,28,28,704]{3,2,1,0:T(8,128)(2,1)} %broadcast_multiply_fusion), channel_id=1, source_target_pairs={{1,0},{2,1},{3,2},{4,3},{5,4},{6,5},{7,6},{8,7},{9,8},{10,9},{11,1... | collective-permute-start | bytes 3311624 | tf_op jit(solution)/shard_map/ppermute | solution.py:10
  12.0 106.8 %collective-permute-start = (bf16[1,28,28,704]{3,2,1,0:T(8,128)(2,1)S(1)}, bf16[1,28,28,704]{3,2,1,0:T(8,128)(2,1)}, u32[]{:S(2)}, u32[]{:S(2)}) collective-permute-start(bf16[1,28,28,704]{3,2,1,0:T(8,128)(2,1)S(1)} %copy-done), channel_id=1, source_target_pairs={{0,1},{1,2},{2,3},{3,4},{4,5},{5,6},{6,7},{7,8},{8,9},{9,10},{10,1... | collective-permute-start | bytes 3311624 | tf_op jit(solution)/shard_map/ppermute | solution.py:10
  50.0 68.8 %copy-start.2 = (bf16[1,28,28,704]{3,2,1,0:T(8,128)(2,1)}, bf16[1,28,28,704]{3,2,1,0:T(8,128)(2,1)S(1)}, u32[]{:S(2)}) copy-start(bf16[1,28,28,704]{3,2,1,0:T(8,128)(2,1)S(1)} %collective-permute-done.1) | copy-start | bytes 3311620
  172.3 28.0 %copy-start.6 = (f32[2816]{0:T(1024)S(1)}, f32[2816]{0:T(1024)}, u32[]{:S(2)}) copy-start(f32[2816]{0:T(1024)} %param.21) | copy-start | bytes 33796
  172.3 28.0 %copy-start.9 = (f32[704]{0:T(1024)S(1)}, f32[704]{0:T(1024)}, u32[]{:S(2)}) copy-start(f32[704]{0:T(1024)} %param.19) | copy-start | bytes 8452
  172.3 28.0 %copy-start.10 = (f32[704]{0:T(1024)S(1)}, f32[704]{0:T(1024)}, u32[]{:S(2)}) copy-start(f32[704]{0:T(1024)} %param.18) | copy-start | bytes 8452
  174.5 192.3 %copy-start.1 = (f32[784,704]{1,0:T(8,128)S(1)}, f32[784,704]{1,0:T(8,128)}, u32[]{:S(2)}) copy-start(f32[784,704]{1,0:T(8,128)} %reshape.250) | copy-start | bytes 6623236
  174.5 192.3 %copy-start.7 = (f32[2816]{0:T(1024)S(1)}, f32[2816]{0:T(1024)}, u32[]{:S(2)}) copy-start(f32[2816]{0:T(1024)} %param.23) | copy-start | bytes 33796
  174.5 192.3 %copy-start.8 = (f32[2816]{0:T(1024)S(1)}, f32[2816]{0:T(1024)}, u32[]{:S(2)}) copy-start(f32[2816]{0:T(1024)} %param.22) | copy-start | bytes 33796
  174.6 192.3 %copy-start.11 = (f32[704]{0:T(1024)S(1)}, f32[704]{0:T(1024)}, u32[]{:S(2)}) copy-start(f32[704]{0:T(1024)} %param.25) | copy-start | bytes 8452
Sparse Core Ops, SparseCore 0:
  9.4 190.8 all-gather.2
  202.4 164.4 all-gather.4
where the time goes:
time: 386 us
  waiting for transfers between devices  264 us (68%)
  other arithmetic  57.1 us (15%)
  matrix products  35 us (9%)
  between operations  14.9 us (4%)
  starting transfers between devices  7.45 us (2%)
  local copies, waits for them, and re-layouts  7.02 us (2%)
    all_gather x1, waiting for transfers between devices, per_device(): whole_down = lax.all_gather(down_weight, 'tm', axis=0, tiled=True)  139 us
    ppermute x2, waiting for transfers between devices, from_behind(): return lax.ppermute(value, axis, pairs)  98.7 us
    reduce_sum x1, other arithmetic, layer_norm(): mean_val = jnp.mean(conv, axis=-1, keepdims=True)  53.5 us
    dot_general x1, matrix products, per_device(): jnp.dot(normed, lax.all_gather(up_weight, 'tm', axis=1, tiled=True), pref...  26.3 us
    all_gather x1, waiting for transfers between devices, per_device(): lax.all_gather(up_weight, 'tm', axis=1, tiled=True)  25.7 us
    dot_general x1, matrix products, per_device(): projected = jnp.dot(grn, whole_down, preferred_element_type=jnp.float32)  8.75 us
  transfers between devices with their start and end apart: 4, of which 4 were waited for; matrix products, arithmetic and copies ran while one was open for 23% of the time, Pallas kernels for 0%

commit v1 on v0

v1 whole, which is shorter than its diff:
```python
import jax
import jax.numpy as jnp
from jax import lax
from jax.experimental import pallas as pl
from jax.experimental.pallas import tpu as pltpu
from jax.sharding import PartitionSpec as P

C, HID, H, W = 704, 2816, 28, 28
PIX = H * W
LANES = 128
CHUNKS = 6
HALF = 384
SHARD = 88
ROWS4 = 4 * SHARD
VMEM = 56 * 1024 * 1024
UP_OFFSETS = ((0, 1, 7, 2), (4, 5, 3, 6))
DOWN_OFFSETS = ((2, 7, 1, 0), (6, 3, 5, 4))

vmem_spec = pl.BlockSpec(memory_space=pltpu.VMEM)
smem_spec = pl.BlockSpec(memory_space=pltpu.SMEM)
any_spec = pl.BlockSpec(memory_space=pl.ANY)


def place():
    v = lax.axis_index("video")
    t = lax.axis_index("tm")
    return v // 4, v % 2, t // 4, t % 4


def pick(table, index):
    value = jnp.int32(table[0])
    for k in range(1, len(table)):
        value = jnp.where(index == k, jnp.int32(table[k]), value)
    return value


def permute(value, source_of):
    pairs = []
    for x in range(4):
        for zh in range(2):
            for c in range(2):
                for y in range(8):
                    for zl in range(4):
                        src = source_of(x, zh, c, y, zl)
                        if src is None:
                            continue
                        pairs.append((flat(*src), flat(x, zh, c, y, zl)))
    return lax.ppermute(value, ("video", "tm"), pairs)


def flat(x, zh, c, y, zl):
    return ((x * 2 + zh) * 2 + c) * 32 + y * 4 + zl


def from_frame(by):
    def source_of(x, zh, c, y, zl):
        t = y * 4 + zl + by
        return (x, zh, c, t // 4, t % 4) if 0 <= t < 32 else None

    return source_of


def widen(value):
    if value.shape[-1] == LANES:
        return value
    zeros = jnp.zeros(value.shape[:-1] + (LANES - value.shape[-1],), value.dtype)
    return jnp.concatenate([value, zeros], axis=-1)


def lanes(chunk):
    return slice(chunk * LANES, min((chunk + 1) * LANES, C))


def flatten_kernel(clip_ref, x_ref, flat_ref, masked_ref):
    keep = (1 - clip_ref[0]).astype(jnp.float32)
    for g in range(7):
        rows = jnp.concatenate([x_ref[4 * g + r].astype(jnp.float32) for r in range(4)], axis=0)
        flat_ref[112 * g : 112 * (g + 1), :] = rows.astype(jnp.bfloat16)
        masked_ref[112 * g : 112 * (g + 1), :] = (rows * keep).astype(jnp.bfloat16)


def flatten(clip, frame):
    out = jax.ShapeDtypeStruct((PIX, C), jnp.bfloat16)
    return pl.pallas_call(
        flatten_kernel,
        out_shape=(out, out),
        in_specs=[smem_spec, vmem_spec],
        out_specs=(vmem_spec, vmem_spec),
        compiler_params=pltpu.CompilerParams(vmem_limit_bytes=VMEM),
        name="flatten",
    )(clip, frame)


def conv_kernel(first, count, x_ref, k_ref, t_ref, b_ref, o_ref, xp, kb, bb):
    xp[...] = jnp.zeros_like(xp)
    for n in range(count):
        part = lanes(first + n)
        for i in range(H):
            xp[n, 3 + i, 3:31, :] = widen(x_ref[i, :, part].astype(jnp.float32))
        for tap in range(49):
            row = widen(k_ref[tap : tap + 1, part])
            if tap == 24:
                row = row + widen(t_ref[1:2, part])
            kb[n, tap] = jnp.broadcast_to(row, (8, LANES))
        bb[n] = jnp.broadcast_to(widen(b_ref[:, part]), (8, LANES))

    def body(step, carry):
        n = step // 7
        g = step % 7
        done = [[None] * 4 for _ in range(4)]
        for jb in range(4):
            acc = [bb[n]] * 4
            for b in range(7):
                xs = [xp[n, 4 * g + q, 8 * jb + b : 8 * jb + b + 8, :] for q in range(10)]
                for a in range(7):
                    kv = kb[n, 7 * a + b]
                    for r in range(4):
                        acc[r] = acc[r] + kv * xs[r + a]
            for r in range(4):
                done[r][jb] = acc[r] if jb < 3 else acc[r][:4]
        rows = jnp.concatenate([done[r][jb] for r in range(4) for jb in range(4)], axis=0)
        o_ref[n, pl.ds(pl.multiple_of(112 * g, 8), 112), :] = rows
        return carry

    lax.fori_loop(0, 7 * count, body, 0)


def conv(first, count, frame, space_kernel, time_kernel, conv_bias):
    return pl.pallas_call(
        lambda *refs: conv_kernel(first, count, *refs),
        out_shape=jax.ShapeDtypeStruct((count, PIX, LANES), jnp.float32),
        in_specs=[vmem_spec] * 4,
        out_specs=vmem_spec,
        scratch_shapes=[
            pltpu.VMEM((count, 34, 40, LANES), jnp.float32),
            pltpu.VMEM((count, 49, 8, LANES), jnp.float32),
            pltpu.VMEM((count, 8, LANES), jnp.float32),
        ],
        compiler_params=pltpu.CompilerParams(vmem_limit_bytes=VMEM),
        name="conv",
    )(frame, space_kernel, time_kernel, conv_bias)


def order_kernel(*refs):
    _, _, _, zl = place()
    blocks, (up_ref, down_ref) = refs[:4], refs[4:]
    for r in range(4):
        up_ref[zl ^ r] = blocks[r][0]
        down_ref[zl ^ r] = blocks[r][1]


def order(blocks):
    out = jax.ShapeDtypeStruct((4, SHARD, HALF), jnp.bfloat16)
    return pl.pallas_call(
        order_kernel,
        out_shape=(out, out),
        in_specs=[vmem_spec] * 4,
        out_specs=(vmem_spec, vmem_spec),
        compiler_params=pltpu.CompilerParams(vmem_limit_bytes=VMEM),
        name="order",
    )(*blocks)


def block_copies(offsets, own, other, weight, sems):
    x, core, y, _ = place()
    copies = []
    for step in range(4):
        for side in range(2):
            row = ((y + pick(offsets[side], (x + step) % 4)) % 8) * ROWS4
            for half, refs in ((core, own), (1 - core, other)):
                copies.append(
                    pltpu.make_async_copy(
                        refs[step].at[side],
                        weight.at[half, pl.ds(pl.multiple_of(row, 32), ROWS4), :],
                        sems.at[len(copies)],
                    )
                )
    return copies


def up_kernel(clip_ref, *refs):
    (c0_ref, c1_ref, prev_ref, next_ref, t_ref, gain_ref, nbias_ref, ubias_ref) = refs[:8]
    own, other = refs[8:12], refs[12:16]
    hid_ref, energy_ref, weight, normed, sems = refs[16:]
    copies = block_copies(UP_OFFSETS, own, other, weight, sems)
    for copy in copies:
        copy.start()
    keep = (1 - clip_ref[0]).astype(jnp.float32)

    def norm_rows(step, carry):
        rows = pl.ds(pl.multiple_of(step * 16, 16), 16)
        parts = []
        for n in range(CHUNKS):
            part = lanes(n)
            base = c0_ref[n, rows, :] if n < 3 else c1_ref[n - 3, rows, :]
            before = widen(prev_ref[rows, part].astype(jnp.float32)) * (widen(t_ref[0:1, part]) * keep)
            after = widen(next_ref[rows, part].astype(jnp.float32)) * widen(t_ref[2:3, part])
            parts.append(base + before + after)
        total = parts[0]
        for n in range(1, CHUNKS):
            total = total + parts[n]
        mean = jnp.sum(total, axis=-1, keepdims=True) * (1.0 / C)
        parts = [p - mean for p in parts]
        lane = lax.broadcasted_iota(jnp.int32, parts[-1].shape, 1)
        parts[-1] = jnp.where(lane < C - 5 * LANES, parts[-1], 0.0)
        total = parts[0] * parts[0]
        for n in range(1, CHUNKS):
            total = total + parts[n] * parts[n]
        var = jnp.sum(total, axis=-1, keepdims=True) * (1.0 / C)
        scale = lax.rsqrt(var + 1e-06)
        for n in range(CHUNKS):
            value = parts[n] * scale * widen(gain_ref[:, lanes(n)]) + widen(nbias_ref[:, lanes(n)])
            normed[rows, n * LANES : (n + 1) * LANES] = value.astype(jnp.bfloat16)
        return carry

    lax.fori_loop(0, PIX // 16, norm_rows, 0)
    for copy in copies:
        copy.wait()

    def units(step, carry):
        cols = pl.ds(pl.multiple_of(step * 256, 256), 256)
        dims = (((1,), (1,)), ((), ()))
        value = lax.dot_general(
            normed[:, :HALF], weight[0, cols, :], dims, preferred_element_type=jnp.float32
        ) + lax.dot_general(
            normed[:, HALF:], weight[1, cols, :], dims, preferred_element_type=jnp.float32
        )
        value = value + ubias_ref[:, cols]
        hid = (0.5 * value * (1.0 + lax.erf(value * 0.7071067811865476))).astype(jnp.bfloat16)
        hid_ref[:, cols] = hid
        wide = hid.astype(jnp.float32)
        energy_ref[:, cols] = jnp.sum(wide * wide, axis=0, keepdims=True)
        return carry

    lax.fori_loop(0, HID // 256, units, 0)


def up(clip, conv0, conv1, prev, nxt, time_kernel, gain, nbias, ubias, own, other):
    return pl.pallas_call(
        up_kernel,
        out_shape=(
            jax.ShapeDtypeStruct((PIX, HID), jnp.bfloat16),
            jax.ShapeDtypeStruct((1, HID), jnp.float32),
        ),
        in_specs=[smem_spec] + [vmem_spec] * 8 + [any_spec] * 8,
        out_specs=(vmem_spec, vmem_spec),
        scratch_shapes=[
            pltpu.VMEM((2, HID, HALF), jnp.bfloat16),
            pltpu.VMEM((PIX, CHUNKS * LANES), jnp.bfloat16),
            pltpu.SemaphoreType.DMA((16,)),
        ],
        compiler_params=pltpu.CompilerParams(vmem_limit_bytes=VMEM),
        name="up",
    )(clip, conv0, conv1, prev, nxt, time_kernel, gain, nbias, ubias, *own, *other)


def down_kernel(hid_ref, energy_ref, gamma_ref, beta_ref, dbias_ref, flat_ref, *refs):
    own, other = refs[:4], refs[4:8]
    out_ref, weight, grn, sums, sems = refs[8:]
    copies = block_copies(DOWN_OFFSETS, own, other, weight, sems)
    for copy in copies:
        copy.start()
    energy = jnp.sqrt(energy_ref[...])
    ratio = energy / (jnp.sum(energy, axis=1, keepdims=True) * (1.0 / HID) + 1e-06)
    grow = gamma_ref[...] * ratio + 1.0

    def scale(step, carry):
        rows = pl.ds(pl.multiple_of(step * 16, 16), 16)
        grn[rows, :] = (hid_ref[rows, :].astype(jnp.float32) * grow + beta_ref[...]).astype(jnp.bfloat16)
        return carry

    lax.fori_loop(0, PIX // 16, scale, 0)
    for copy in copies:
        copy.wait()
    for half in range(2):
        width = min(HALF, C - half * HALF)
        cols = slice(half * HALF, half * HALF + width)
        value = jnp.dot(grn[...], weight[half], preferred_element_type=jnp.float32)
        sums[:, cols] = value[:, :width]
    for g in range(7):
        rows = slice(112 * g, 112 * (g + 1))
        value = sums[rows, :] + dbias_ref[...] + flat_ref[rows, :].astype(jnp.float32)
        for r in range(4):
            out_ref[4 * g + r] = value[28 * r : 28 * (r + 1)].astype(jnp.bfloat16)


def down(hid, energy, gamma, beta, dbias, flat_frame, own, other):
    return pl.pallas_call(
        down_kernel,
        out_shape=jax.ShapeDtypeStruct((H, W, C), jnp.bfloat16),
        in_specs=[vmem_spec] * 6 + [any_spec] * 8,
        out_specs=vmem_spec,
        scratch_shapes=[
            pltpu.VMEM((2, HID, HALF), jnp.bfloat16),
            pltpu.VMEM((PIX, HID), jnp.bfloat16),
            pltpu.VMEM((PIX, C), jnp.float32),
            pltpu.SemaphoreType.DMA((16,)),
        ],
        compiler_params=pltpu.CompilerParams(vmem_limit_bytes=VMEM),
        name="down",
    )(hid, energy, gamma, beta, dbias, flat_frame, *own, *other)


def spread_z(up_weight, down_weight):
    core = lax.axis_index("video") % 2
    both = jnp.stack([up_weight.T, down_weight])
    both = jnp.pad(both, ((0, 0), (0, 0), (0, 2 * HALF - C)))
    mine = lax.dynamic_slice(both, (0, 0, core * HALF), (2, SHARD, HALF))
    blocks = [mine]
    for r in range(1, 4):
        blocks.append(permute(mine, lambda x, zh, c, y, zl: (x, zh, c, y, zl ^ r)))
    return order(blocks)


def spread_y(block, offsets):
    block = block.reshape(ROWS4, HALF)
    sides = [
        permute(block, lambda x, zh, c, y, zl: (x, zh, c, (y + side[x]) % 8, zl)) for side in offsets
    ]
    return jnp.stack(sides)


def spread_x(block):
    return [permute(block, lambda x, zh, c, y, zl: ((x + by) % 4, zh, c, y, zl)) for by in range(1, 4)]


def swap_core(block):
    return permute(block, lambda x, zh, c, y, zl: (x, zh, 1 - c, y, zl))


def per_device(
    frames,
    clip_cut,
    space_kernel,
    time_kernel,
    conv_bias,
    norm_gain,
    norm_bias,
    up_weight,
    up_bias,
    grn_gamma,
    grn_beta,
    down_weight,
    down_bias,
):
    frame = frames[0]
    row = lambda value: value[None]
    up4, down4 = spread_z(up_weight, down_weight)
    flat_frame, masked = flatten(clip_cut, frame)
    prev = permute(flat_frame, from_frame(-1))
    nxt = permute(masked, from_frame(1))
    up_y = spread_y(up4, UP_OFFSETS)
    down_y = spread_y(down4, DOWN_OFFSETS)
    conv0 = conv(0, 3, frame, space_kernel, time_kernel, row(conv_bias))
    conv1 = conv(3, 3, frame, space_kernel, time_kernel, row(conv_bias))
    up_own = [up_y] + spread_x(up_y)
    up_other = [swap_core(block) for block in up_own]
    down_own = [down_y] + spread_x(down_y)
    down_other = [swap_core(block) for block in down_own]
    hid, energy = up(
        clip_cut,
        conv0,
        conv1,
        prev,
        nxt,
        time_kernel,
        row(norm_gain),
        row(norm_bias),
        row(up_bias),
        up_own,
        up_other,
    )
    out = down(
        hid, energy, row(grn_gamma), row(grn_beta), row(down_bias), flat_frame, down_own, down_other
    )
    return out[None]


def solution(mesh):
    return jax.shard_map(
        per_device,
        mesh=mesh,
        in_specs=(
            P(("video", "tm"), None, None, None),
            P(("video", "tm")),
            P(),
            P(),
            P(),
            P(),
            P(),
            P(None, "tm"),
            P(),
            P(),
            P(),
            P("tm", None),
            P(),
        ),
        out_specs=P(("video", "tm"), None, None, None),
        check_vma=False,
    )
```

time: 386 us -> 202 us (0.52)
  the two profiles are of different devices: /device:TPU:2 before, /device:TPU:73 now
where the time goes in v1:
time: 202 us
  starting transfers between devices  83.5 us (41%)
  Pallas kernels  57.5 us (28%)
  waiting for transfers between devices  51.7 us (26%)
  local copies, waits for them, and re-layouts  6.49 us (3%)
    ppermute x23, starting transfers between devices, permute(): return lax.ppermute(value, ('video', 'tm'), pairs)  83.5 us
    ppermute x23, waiting for transfers between devices, permute(): return lax.ppermute(value, ('video', 'tm'), pairs)  51.7 us
    pallas_call x1, Pallas kernels, up(): pl.pallas_call(up_kernel, out_shape=(jax.ShapeDtypeStruct((PIX, HID), jnp...  22.6 us
    pallas_call x2, Pallas kernels, conv(): pl.pallas_call(lambda *refs: conv_kernel(first, count, *refs), out_shape=...  19.1 us
    pallas_call x1, Pallas kernels, down(): pl.pallas_call(down_kernel, out_shape=jax.ShapeDtypeStruct((H, W, C), jnp...  10.9 us
    broadcast_in_dim x7, local copies, waits for them, and re-layouts, per_device(): row = lambda value: value[None]  4.18 us
  transfers between devices with their start and end apart: 23, of which 8 were waited for; matrix products, arithmetic and copies ran while one was open for 2% of the time, Pallas kernels for 22%

profile of v1, /device:TPU:73, one launch (start us, length us, event | category | flops | bytes accessed | tf_op | source)
XLA Modules:
  0.0 201.5 jit_solution(6734857750224032615)
XLA Ops:
  0.0 1.0 fusion.2.refs_0_
  1.0 1.9 collective-permute-start.2
  2.9 5.8 %collective-permute-start.3 = (bf16[2,88,384]{2,1,0:T(8,128)(2,1)S(1)}, bf16[2,88,384]{2,1,0:T(8,128)(2,1)S(1)}, u32[]{:S(2)}, u32[]{:S(2)}) collective-permute-start(bf16[2,88,384]{2,1,0:T(8,128)(2,1)S(1)} %fusion.2.refs_0_), channel_id=1, source_target_pairs={{2,0},{3,1},{0,2},{1,3},{6,4},{7,5},{4,6},{5,7},{10,8},{11,9},{8,1... | collective-permute-start | bytes 405512 | tf_op jit(solution)/shard_map/ppermute | solution.py:48
  8.7 2.2 %collective-permute-start.4 = (bf16[2,88,384]{2,1,0:T(8,128)(2,1)S(1)}, bf16[2,88,384]{2,1,0:T(8,128)(2,1)S(1)}, u32[]{:S(2)}, u32[]{:S(2)}) collective-permute-start(bf16[2,88,384]{2,1,0:T(8,128)(2,1)S(1)} %fusion.2.refs_0_), channel_id=1, source_target_pairs={{3,0},{2,1},{1,2},{0,3},{7,4},{6,5},{5,6},{4,7},{11,8},{10,9},{9,1... | collective-permute-start | bytes 405512 | tf_op jit(solution)/shard_map/ppermute | solution.py:48
  10.9 5.7 %collective-permute-done.3.refs_2_ = bf16[2,88,384]{2,1,0:T(8,128)(2,1)S(1)} collective-permute-done((bf16[2,88,384]{2,1,0:T(8,128)(2,1)S(1)}, bf16[2,88,384]{2,1,0:T(8,128)(2,1)S(1)}, u32[]{:S(2)}, u32[]{:S(2)}) %collective-permute-start.3) | collective-permute-done | bytes 135200 | tf_op jit(solution)/shard_map/ppermute | solution.py:48
  16.6 4.5 %collective-permute-done.4.refs_3_ = bf16[2,88,384]{2,1,0:T(8,128)(2,1)S(1)} collective-permute-done((bf16[2,88,384]{2,1,0:T(8,128)(2,1)S(1)}, bf16[2,88,384]{2,1,0:T(8,128)(2,1)S(1)}, u32[]{:S(2)}, u32[]{:S(2)}) %collective-permute-start.4) | collective-permute-done | bytes 135200 | tf_op jit(solution)/shard_map/ppermute | solution.py:48
  21.2 0.6 copy-done.17
  21.8 1.9 order.1
  23.8 1.6 collective-permute-start.5
  25.4 6.5 %collective-permute-start.6 = (bf16[352,384]{1,0:T(8,128)(2,1)}, bf16[352,384]{1,0:T(8,128)(2,1)S(1)}, u32[]{:S(2)}, u32[]{:S(2)}) collective-permute-start(bf16[352,384]{1,0:T(8,128)(2,1)} %bitcast.24), channel_id=1, source_target_pairs={{16,0},{17,1},{18,2},{19,3},{20,4},{21,5},{22,6},{23,7},{24,8},{25... | collective-permute-start | bytes 811016 | tf_op jit(solution)/shard_map/ppermute | solution.py:48
  31.9 9.1 %collective-permute-done.6 = bf16[352,384]{1,0:T(8,128)(2,1)S(1)} collective-permute-done((bf16[352,384]{1,0:T(8,128)(2,1)}, bf16[352,384]{1,0:T(8,128)(2,1)S(1)}, u32[]{:S(2)}, u32[]{:S(2)}) %collective-permute-start.6) | collective-permute-done | bytes 270368 | tf_op jit(solution)/shard_map/ppermute | solution.py:48
  41.1 9.2 %collective-permute-start.7 = (bf16[2,352,384]{2,1,0:T(8,128)(2,1)S(1)}, bf16[2,352,384]{2,1,0:T(8,128)(2,1)S(1)}, u32[]{:S(2)}, u32[]{:S(2)}) collective-permute-start(bf16[2,352,384]{2,1,0:T(8,128)(2,1)S(1)} %pad_maximum_fusion.refs_8_), channel_id=1, source_target_pairs={{128,0},{129,1},{130,2},{131,3},{132,4},{133,5},{134,6},{135,7},{1... | collective-permute-start | bytes 1622024 | tf_op jit(solution)/shard_map/ppermute | solution.py:48
  50.3 4.7 %collective-permute-start.8 = (bf16[2,352,384]{2,1,0:T(8,128)(2,1)S(1)}, bf16[2,352,384]{2,1,0:T(8,128)(2,1)S(1)}, u32[]{:S(2)}, u32[]{:S(2)}) collective-permute-start(bf16[2,352,384]{2,1,0:T(8,128)(2,1)S(1)} %pad_maximum_fusion.refs_8_), channel_id=1, source_target_pairs={{256,0},{257,1},{258,2},{259,3},{260,4},{261,5},{262,6},{263,7},{2... | collective-permute-start | bytes 1622024 | tf_op jit(solution)/shard_map/ppermute | solution.py:48
  55.0 1.9 collective-permute-start.9
  57.0 6.7 %collective-permute-start.14 = (bf16[352,384]{1,0:T(8,128)(2,1)}, bf16[352,384]{1,0:T(8,128)(2,1)S(1)}, u32[]{:S(2)}, u32[]{:S(2)}) collective-permute-start(bf16[352,384]{1,0:T(8,128)(2,1)} %bitcast.21), channel_id=1, source_target_pairs={{8,0},{9,1},{10,2},{11,3},{12,4},{13,5},{14,6},{15,7},{16,8},{17,9... | collective-permute-start | bytes 811016 | tf_op jit(solution)/shard_map/ppermute | solution.py:48
  63.7 3.9 %collective-permute-start.15 = (bf16[352,384]{1,0:T(8,128)(2,1)}, bf16[352,384]{1,0:T(8,128)(2,1)S(1)}, u32[]{:S(2)}, u32[]{:S(2)}) collective-permute-start(bf16[352,384]{1,0:T(8,128)(2,1)} %bitcast.22), channel_id=1, source_target_pairs={{24,0},{25,1},{26,2},{27,3},{28,4},{29,5},{30,6},{31,7},{0,8},{1,9... | collective-permute-start | bytes 811016 | tf_op jit(solution)/shard_map/ppermute | solution.py:48
  68.3 3.1 %flatten.1 = (bf16[784,704]{1,0:T(8,128)(2,1)}, bf16[784,704]{1,0:T(8,128)(2,1)}) custom-call(s32[1]{0:T(128)S(6)} %copy.14.clip_ref, bf16[28,28,704]{2,1,0:T(8,128)(2,1)} %bitcast.12), custom_call_target="tpu_custom_call" | custom-call | tf_op jit(solution)/shard_map/flatten/pallas_call | solution.py:84
  71.3 7.1 %collective-permute-done.14 = bf16[352,384]{1,0:T(8,128)(2,1)S(1)} collective-permute-done((bf16[352,384]{1,0:T(8,128)(2,1)}, bf16[352,384]{1,0:T(8,128)(2,1)S(1)}, u32[]{:S(2)}, u32[]{:S(2)}) %collective-permute-start.14) | collective-permute-done | bytes 270368 | tf_op jit(solution)/shard_map/ppermute | solution.py:48
  78.5 1.9 collective-permute-start
  80.4 3.4 %collective-permute-start.1 = (bf16[784,704]{1,0:T(8,128)(2,1)}, bf16[784,704]{1,0:T(8,128)(2,1)S(1)}, u32[]{:S(2)}, u32[]{:S(2)}) collective-permute-start(bf16[784,704]{1,0:T(8,128)(2,1)} %get-tuple-element.12), channel_id=1, source_target_pairs={{1,0},{2,1},{3,2},{4,3},{5,4},{6,5},{7,6},{8,7},{9,8},{10,9},{11,1... | collective-permute-start | bytes 3311624 | tf_op jit(solution)/shard_map/ppermute | solution.py:48
  83.8 3.1 %collective-permute-start.10 = (bf16[2,352,384]{2,1,0:T(8,128)(2,1)S(1)}, bf16[2,352,384]{2,1,0:T(8,128)(2,1)S(1)}, u32[]{:S(2)}, u32[]{:S(2)}) collective-permute-start(bf16[2,352,384]{2,1,0:T(8,128)(2,1)S(1)} %pad_maximum_fusion.refs_8_), channel_id=1, source_target_pairs={{32,0},{33,1},{34,2},{35,3},{36,4},{37,5},{38,6},{39,7},{40,8},{41... | collective-permute-start | bytes 1622024 | tf_op jit(solution)/shard_map/ppermute | solution.py:48
  87.0 1.9 collective-permute-start.16
  88.9 9.6 %collective-permute-start.17 = (bf16[2,352,384]{2,1,0:T(8,128)(2,1)S(1)}, bf16[2,352,384]{2,1,0:T(8,128)(2,1)S(1)}, u32[]{:S(2)}, u32[]{:S(2)}) collective-permute-start(bf16[2,352,384]{2,1,0:T(8,128)(2,1)S(1)} %pad_maximum_fusion.1.refs_0_), channel_id=1, source_target_pairs={{256,0},{257,1},{258,2},{259,3},{260,4},{261,5},{262,6},{263,7},{2... | collective-permute-start | bytes 1622024 | tf_op jit(solution)/shard_map/ppermute | solution.py:48
  98.6 2.8 %collective-permute-start.18 = (bf16[2,352,384]{2,1,0:T(8,128)(2,1)S(1)}, bf16[2,352,384]{2,1,0:T(8,128)(2,1)S(1)}, u32[]{:S(2)}, u32[]{:S(2)}) collective-permute-start(bf16[2,352,384]{2,1,0:T(8,128)(2,1)S(1)} %pad_maximum_fusion.1.refs_0_), channel_id=1, source_target_pairs={{384,0},{385,1},{386,2},{387,3},{388,4},{389,5},{390,6},{391,7},{3... | collective-permute-start | bytes 1622024 | tf_op jit(solution)/shard_map/ppermute | solution.py:48
  101.3 3.3 %collective-permute-done.16.refs_1_ = bf16[2,352,384]{2,1,0:T(8,128)(2,1)S(1)} collective-permute-done((bf16[2,352,384]{2,1,0:T(8,128)(2,1)S(1)}, bf16[2,352,384]{2,1,0:T(8,128)(2,1)S(1)}, u32[]{:S(2)}, u32[]{:S(2)}) %collective-permute-start.16) | collective-permute-done | bytes 540704 | tf_op jit(solution)/shard_map/ppermute | solution.py:48
  104.6 2.7 %collective-permute-start.11 = (bf16[2,352,384]{2,1,0:T(8,128)(2,1)S(1)}, bf16[2,352,384]{2,1,0:T(8,128)(2,1)S(1)}, u32[]{:S(2)}, u32[]{:S(2)}) collective-permute-start(bf16[2,352,384]{2,1,0:T(8,128)(2,1)S(1)} %collective-permute-done.7.refs_9_), channel_id=1, source_target_pairs={{32,0},{33,1},{34,2},{35,3},{36,4},{37,5},{38,6},{39,7},{40,8},{41... | collective-permute-start | bytes 1622024 | tf_op jit(solution)/shard_map/ppermute | solution.py:48
  107.3 3.9 %collective-permute-done.17.refs_2_ = bf16[2,352,384]{2,1,0:T(8,128)(2,1)S(1)} collective-permute-done((bf16[2,352,384]{2,1,0:T(8,128)(2,1)S(1)}, bf16[2,352,384]{2,1,0:T(8,128)(2,1)S(1)}, u32[]{:S(2)}, u32[]{:S(2)}) %collective-permute-start.17) | collective-permute-done | bytes 540704 | tf_op jit(solution)/shard_map/ppermute | solution.py:48
  111.2 2.7 %collective-permute-start.12 = (bf16[2,352,384]{2,1,0:T(8,128)(2,1)S(1)}, bf16[2,352,384]{2,1,0:T(8,128)(2,1)S(1)}, u32[]{:S(2)}, u32[]{:S(2)}) collective-permute-start(bf16[2,352,384]{2,1,0:T(8,128)(2,1)S(1)} %collective-permute-done.8.refs_10_), channel_id=1, source_target_pairs={{32,0},{33,1},{34,2},{35,3},{36,4},{37,5},{38,6},{39,7},{40,8},{41... | collective-permute-start | bytes 1622024 | tf_op jit(solution)/shard_map/ppermute | solution.py:48
  113.9 9.0 %collective-permute-done.18.refs_3_ = bf16[2,352,384]{2,1,0:T(8,128)(2,1)S(1)} collective-permute-done((bf16[2,352,384]{2,1,0:T(8,128)(2,1)S(1)}, bf16[2,352,384]{2,1,0:T(8,128)(2,1)S(1)}, u32[]{:S(2)}, u32[]{:S(2)}) %collective-permute-start.18) | collective-permute-done | bytes 540704 | tf_op jit(solution)/shard_map/ppermute | solution.py:48
  122.9 2.4 %collective-permute-start.19 = (bf16[2,352,384]{2,1,0:T(8,128)(2,1)S(1)}, bf16[2,352,384]{2,1,0:T(8,128)(2,1)S(1)}, u32[]{:S(2)}, u32[]{:S(2)}) collective-permute-start(bf16[2,352,384]{2,1,0:T(8,128)(2,1)S(1)} %pad_maximum_fusion.1.refs_0_), channel_id=1, source_target_pairs={{32,0},{33,1},{34,2},{35,3},{36,4},{37,5},{38,6},{39,7},{40,8},{41... | collective-permute-start | bytes 1622024 | tf_op jit(solution)/shard_map/ppermute | solution.py:48
  125.2 9.1 %collective-permute-done.refs_2_ = bf16[784,704]{1,0:T(8,128)(2,1)S(1)} collective-permute-done((bf16[784,704]{1,0:T(8,128)(2,1)}, bf16[784,704]{1,0:T(8,128)(2,1)S(1)}, u32[]{:S(2)}, u32[]{:S(2)}) %collective-permute-start) | collective-permute-done | bytes 1103904 | tf_op jit(solution)/shard_map/ppermute | solution.py:48
  134.3 2.4 %collective-permute-start.13 = (bf16[2,352,384]{2,1,0:T(8,128)(2,1)S(1)}, bf16[2,352,384]{2,1,0:T(8,128)(2,1)}, u32[]{:S(2)}, u32[]{:S(2)}) collective-permute-start(bf16[2,352,384]{2,1,0:T(8,128)(2,1)S(1)} %collective-permute-done.9.refs_11_), channel_id=1, source_target_pairs={{32,0},{33,1},{34,2},{35,3},{36,4},{37,5},{38,6},{39,7},{40,8},{41... | collective-permute-start | bytes 1622024 | tf_op jit(solution)/shard_map/ppermute | solution.py:48
  136.7 1.9 collective-permute-start.20
  138.7 2.4 %collective-permute-start.21 = (bf16[2,352,384]{2,1,0:T(8,128)(2,1)S(1)}, bf16[2,352,384]{2,1,0:T(8,128)(2,1)}, u32[]{:S(2)}, u32[]{:S(2)}) collective-permute-start(bf16[2,352,384]{2,1,0:T(8,128)(2,1)S(1)} %collective-permute-done.17.refs_2_), channel_id=1, source_target_pairs={{32,0},{33,1},{34,2},{35,3},{36,4},{37,5},{38,6},{39,7},{40,8},{41... | collective-permute-start | bytes 1622024 | tf_op jit(solution)/shard_map/ppermute | solution.py:48
  141.1 0.8 copy-done.14
  141.9 1.9 collective-permute-start.22
  143.8 0.6 broadcast_in_dim.25.refs_3_
  144.4 9.5 %conv.2.refs_0_ = f32[3,784,128]{2,1,0:T(8,128)} custom-call(bf16[28,28,704]{2,1,0:T(8,128)(2,1)} %bitcast.13, f32[49,704]{1,0:T(8,128)} %refs_1_.3, f32[3,704]{1,0:T(4,128)} %refs_4_.1, f32[1,704]{1,0:T(1,128)} %broadcast_in_dim.25.refs_3_), custom_call_target="tpu_custom_call" | custom-call | tf_op jit(solution)/shard_map/conv/pallas_call | solution.py:129
  154.0 9.6 %conv.3.refs_1_ = f32[3,784,128]{2,1,0:T(8,128)} custom-call(bf16[28,28,704]{2,1,0:T(8,128)(2,1)} %bitcast.14, f32[49,704]{1,0:T(8,128)} %refs_1_.3, f32[3,704]{1,0:T(4,128)} %refs_4_.1, f32[1,704]{1,0:T(1,128)} %broadcast_in_dim.25.refs_3_), custom_call_target="tpu_custom_call" | custom-call | tf_op jit(solution)/shard_map/conv/pallas_call | solution.py:129
  163.6 0.6 broadcast_in_dim.28.refs_7_
  164.2 0.6 broadcast_in_dim.26.refs_5_
  164.8 0.6 broadcast_in_dim.27.refs_6_
  165.4 0.6 broadcast_in_dim.29.gamma_ref
  166.0 0.6 broadcast_in_dim.30.beta_ref
  166.6 0.6 broadcast_in_dim.31.dbias_ref
  167.2 22.6 %up.1 = (bf16[784,2816]{1,0:T(8,128)(2,1)}, f32[1,2816]{1,0:T(1,128)}) custom-call(s32[1]{0:T(128)S(6)} %copy.14.clip_ref, f32[3,784,128]{2,1,0:T(8,128)} %conv.2.refs_0_, f32[3,784,128]{2,1,0:T(8,128)} %conv.3.refs_1_, bf16[784,704]{1,0:T(8,128)(2,1)} %copy-done.2, bf16[784,704]{1,0:T(8,128)(2,1)} %copy-done.3, f32[3,704]{1,0:T(4,128)} %refs_4_.1, ...), custom_call_target="tpu_custom_call" | custom-call | tf_op jit(solution)/shard_map/up/pallas_call | solution.py:239
  189.9 0.8 copy-done.12
  190.7 10.9 %down.1 = bf16[28,28,704]{2,1,0:T(8,128)(2,1)} custom-call(bf16[784,2816]{1,0:T(8,128)(2,1)} %get-tuple-element.14.hid_ref, f32[1,2816]{1,0:T(1,128)} %get-tuple-element.15.energy_ref, f32[1,2816]{1,0:T(1,128)} %broadcast_in_dim.29.gamma_ref, f32[1,2816]{1,0:T(1,128)} %broadcast_in_dim.30.beta_ref, f32[1,704]{1,0:T(1,128)} %broadcast_in_dim.31.dbias_ref, ...), custom_call_target="tpu_custom_call" | custom-call | tf_op jit(solution)/shard_map/down/pallas_call | solution.py:288
  (64 shorter events, 0.3 us)
Async XLA Ops:
  1.0 20.2 %copy-start.4 = (bf16[2,88,384]{2,1,0:T(8,128)(2,1)}, bf16[2,88,384]{2,1,0:T(8,128)(2,1)S(1)}, u32[]{:S(2)}) copy-start(bf16[2,88,384]{2,1,0:T(8,128)(2,1)S(1)} %fusion.2.refs_0_) | copy-start | bytes 405508
  1.0 9.9 %collective-permute-start.2 = (bf16[2,88,384]{2,1,0:T(8,128)(2,1)S(1)}, bf16[2,88,384]{2,1,0:T(8,128)(2,1)S(1)}, u32[]{:S(2)}, u32[]{:S(2)}) collective-permute-start(bf16[2,88,384]{2,1,0:T(8,128)(2,1)S(1)} %fusion.2.refs_0_), channel_id=1, source_target_pairs={{1,0},{0,1},{3,2},{2,3},{5,4},{4,5},{7,6},{6,7},{9,8},{8,9},{11,10... | collective-permute-start | bytes 405512 | tf_op jit(solution)/shard_map/ppermute | solution.py:48
  2.9 13.7 %collective-permute-start.3 = (bf16[2,88,384]{2,1,0:T(8,128)(2,1)S(1)}, bf16[2,88,384]{2,1,0:T(8,128)(2,1)S(1)}, u32[]{:S(2)}, u32[]{:S(2)}) collective-permute-start(bf16[2,88,384]{2,1,0:T(8,128)(2,1)S(1)} %fusion.2.refs_0_), channel_id=1, source_target_pairs={{2,0},{3,1},{0,2},{1,3},{6,4},{7,5},{4,6},{5,7},{10,8},{11,9},{8,1... | collective-permute-start | bytes 405512 | tf_op jit(solution)/shard_map/ppermute | solution.py:48
  8.7 12.4 %collective-permute-start.4 = (bf16[2,88,384]{2,1,0:T(8,128)(2,1)S(1)}, bf16[2,88,384]{2,1,0:T(8,128)(2,1)S(1)}, u32[]{:S(2)}, u32[]{:S(2)}) collective-permute-start(bf16[2,88,384]{2,1,0:T(8,128)(2,1)S(1)} %fusion.2.refs_0_), channel_id=1, source_target_pairs={{3,0},{2,1},{1,2},{0,3},{7,4},{6,5},{5,6},{4,7},{11,8},{10,9},{9,1... | collective-permute-start | bytes 405512 | tf_op jit(solution)/shard_map/ppermute | solution.py:48
  10.9 10.2 %copy-start.15 = (bf16[2,88,384]{2,1,0:T(8,128)(2,1)}, bf16[2,88,384]{2,1,0:T(8,128)(2,1)S(1)}, u32[]{:S(2)}) copy-start(bf16[2,88,384]{2,1,0:T(8,128)(2,1)S(1)} %collective-permute-done.2.refs_1_) | copy-start | bytes 405508
  16.6 4.5 %copy-start.16 = (bf16[2,88,384]{2,1,0:T(8,128)(2,1)}, bf16[2,88,384]{2,1,0:T(8,128)(2,1)S(1)}, u32[]{:S(2)}) copy-start(bf16[2,88,384]{2,1,0:T(8,128)(2,1)S(1)} %collective-permute-done.3.refs_2_) | copy-start | bytes 405508
  21.2 0.7 copy-start.17
  23.8 8.2 %collective-permute-start.5 = (bf16[352,384]{1,0:T(8,128)(2,1)}, bf16[352,384]{1,0:T(8,128)(2,1)S(1)}, u32[]{:S(2)}, u32[]{:S(2)}) collective-permute-start(bf16[352,384]{1,0:T(8,128)(2,1)} %bitcast.23), channel_id=1, source_target_pairs={{0,0},{1,1},{2,2},{3,3},{4,4},{5,5},{6,6},{7,7},{8,8},{9,9},{10,10... | collective-permute-start | bytes 811016 | tf_op jit(solution)/shard_map/ppermute | solution.py:48
  25.4 15.7 %collective-permute-start.6 = (bf16[352,384]{1,0:T(8,128)(2,1)}, bf16[352,384]{1,0:T(8,128)(2,1)S(1)}, u32[]{:S(2)}, u32[]{:S(2)}) collective-permute-start(bf16[352,384]{1,0:T(8,128)(2,1)} %bitcast.24), channel_id=1, source_target_pairs={{16,0},{17,1},{18,2},{19,3},{20,4},{21,5},{22,6},{23,7},{24,8},{25... | collective-permute-start | bytes 811016 | tf_op jit(solution)/shard_map/ppermute | solution.py:48
  41.1 45.9 %copy-start = (bf16[2,352,384]{2,1,0:T(8,128)(2,1)}, bf16[2,352,384]{2,1,0:T(8,128)(2,1)S(1)}, u32[]{:S(2)}) copy-start(bf16[2,352,384]{2,1,0:T(8,128)(2,1)S(1)} %pad_maximum_fusion.refs_8_) | copy-start | bytes 1622020
  41.1 42.6 %collective-permute-start.7 = (bf16[2,352,384]{2,1,0:T(8,128)(2,1)S(1)}, bf16[2,352,384]{2,1,0:T(8,128)(2,1)S(1)}, u32[]{:S(2)}, u32[]{:S(2)}) collective-permute-start(bf16[2,352,384]{2,1,0:T(8,128)(2,1)S(1)} %pad_maximum_fusion.refs_8_), channel_id=1, source_target_pairs={{128,0},{129,1},{130,2},{131,3},{132,4},{133,5},{134,6},{135,7},{1... | collective-permute-start | bytes 1622024 | tf_op jit(solution)/shard_map/ppermute | solution.py:48
  50.3 36.7 %collective-permute-start.8 = (bf16[2,352,384]{2,1,0:T(8,128)(2,1)S(1)}, bf16[2,352,384]{2,1,0:T(8,128)(2,1)S(1)}, u32[]{:S(2)}, u32[]{:S(2)}) collective-permute-start(bf16[2,352,384]{2,1,0:T(8,128)(2,1)S(1)} %pad_maximum_fusion.refs_8_), channel_id=1, source_target_pairs={{256,0},{257,1},{258,2},{259,3},{260,4},{261,5},{262,6},{263,7},{2... | collective-permute-start | bytes 1622024 | tf_op jit(solution)/shard_map/ppermute | solution.py:48
  55.0 33.9 %collective-permute-start.9 = (bf16[2,352,384]{2,1,0:T(8,128)(2,1)S(1)}, bf16[2,352,384]{2,1,0:T(8,128)(2,1)S(1)}, u32[]{:S(2)}, u32[]{:S(2)}) collective-permute-start(bf16[2,352,384]{2,1,0:T(8,128)(2,1)S(1)} %pad_maximum_fusion.refs_8_), channel_id=1, source_target_pairs={{384,0},{385,1},{386,2},{387,3},{388,4},{389,5},{390,6},{391,7},{3... | collective-permute-start | bytes 1622024 | tf_op jit(solution)/shard_map/ppermute | solution.py:48
  57.0 21.5 %collective-permute-start.14 = (bf16[352,384]{1,0:T(8,128)(2,1)}, bf16[352,384]{1,0:T(8,128)(2,1)S(1)}, u32[]{:S(2)}, u32[]{:S(2)}) collective-permute-start(bf16[352,384]{1,0:T(8,128)(2,1)} %bitcast.21), channel_id=1, source_target_pairs={{8,0},{9,1},{10,2},{11,3},{12,4},{13,5},{14,6},{15,7},{16,8},{17,9... | collective-permute-start | bytes 811016 | tf_op jit(solution)/shard_map/ppermute | solution.py:48
  63.7 16.7 %collective-permute-start.15 = (bf16[352,384]{1,0:T(8,128)(2,1)}, bf16[352,384]{1,0:T(8,128)(2,1)S(1)}, u32[]{:S(2)}, u32[]{:S(2)}) collective-permute-start(bf16[352,384]{1,0:T(8,128)(2,1)} %bitcast.22), channel_id=1, source_target_pairs={{24,0},{25,1},{26,2},{27,3},{28,4},{29,5},{30,6},{31,7},{0,8},{1,9... | collective-permute-start | bytes 811016 | tf_op jit(solution)/shard_map/ppermute | solution.py:48
  68.2 75.6 %copy-start.21 = (f32[704]{0:T(1024)S(1)}, f32[704]{0:T(1024)}, u32[]{:S(2)}) copy-start(f32[704]{0:T(1024)} %param.17) | copy-start | bytes 8452
  78.5 55.9 %collective-permute-start = (bf16[784,704]{1,0:T(8,128)(2,1)}, bf16[784,704]{1,0:T(8,128)(2,1)S(1)}, u32[]{:S(2)}, u32[]{:S(2)}) collective-permute-start(bf16[784,704]{1,0:T(8,128)(2,1)} %get-tuple-element.11.flat_ref), channel_id=1, source_target_pairs={{0,1},{1,2},{2,3},{3,4},{4,5},{5,6},{6,7},{7,8},{8,9},{9,10},{10,1... | collective-permute-start | bytes 3311624 | tf_op jit(solution)/shard_map/ppermute | solution.py:48
  80.4 56.3 %collective-permute-start.1 = (bf16[784,704]{1,0:T(8,128)(2,1)}, bf16[784,704]{1,0:T(8,128)(2,1)S(1)}, u32[]{:S(2)}, u32[]{:S(2)}) collective-permute-start(bf16[784,704]{1,0:T(8,128)(2,1)} %get-tuple-element.12), channel_id=1, source_target_pairs={{1,0},{2,1},{3,2},{4,3},{5,4},{6,5},{7,6},{8,7},{9,8},{10,9},{11,1... | collective-permute-start | bytes 3311624 | tf_op jit(solution)/shard_map/ppermute | solution.py:48
  83.8 70.2 %copy-start.5 = (bf16[2,352,384]{2,1,0:T(8,128)(2,1)}, bf16[2,352,384]{2,1,0:T(8,128)(2,1)S(1)}, u32[]{:S(2)}) copy-start(bf16[2,352,384]{2,1,0:T(8,128)(2,1)S(1)} %collective-permute-done.7.refs_9_) | copy-start | bytes 1622020
  83.8 14.8 %collective-permute-start.10 = (bf16[2,352,384]{2,1,0:T(8,128)(2,1)S(1)}, bf16[2,352,384]{2,1,0:T(8,128)(2,1)S(1)}, u32[]{:S(2)}, u32[]{:S(2)}) collective-permute-start(bf16[2,352,384]{2,1,0:T(8,128)(2,1)S(1)} %pad_maximum_fusion.refs_8_), channel_id=1, source_target_pairs={{32,0},{33,1},{34,2},{35,3},{36,4},{37,5},{38,6},{39,7},{40,8},{41... | collective-permute-start | bytes 1622024 | tf_op jit(solution)/shard_map/ppermute | solution.py:48
  87.0 66.9 %copy-start.1 = (bf16[2,352,384]{2,1,0:T(8,128)(2,1)}, bf16[2,352,384]{2,1,0:T(8,128)(2,1)S(1)}, u32[]{:S(2)}) copy-start(bf16[2,352,384]{2,1,0:T(8,128)(2,1)S(1)} %pad_maximum_fusion.1.refs_0_) | copy-start | bytes 1622020
  87.0 66.9 %copy-start.6 = (bf16[2,352,384]{2,1,0:T(8,128)(2,1)}, bf16[2,352,384]{2,1,0:T(8,128)(2,1)S(1)}, u32[]{:S(2)}) copy-start(bf16[2,352,384]{2,1,0:T(8,128)(2,1)S(1)} %collective-permute-done.8.refs_10_) | copy-start | bytes 1622020
  87.0 17.6 %collective-permute-start.16 = (bf16[2,352,384]{2,1,0:T(8,128)(2,1)S(1)}, bf16[2,352,384]{2,1,0:T(8,128)(2,1)S(1)}, u32[]{:S(2)}, u32[]{:S(2)}) collective-permute-start(bf16[2,352,384]{2,1,0:T(8,128)(2,1)S(1)} %pad_maximum_fusion.1.refs_0_), channel_id=1, source_target_pairs={{128,0},{129,1},{130,2},{131,3},{132,4},{133,5},{134,6},{135,7},{1... | collective-permute-start | bytes 1622024 | tf_op jit(solution)/shard_map/ppermute | solution.py:48
  88.9 78.3 %copy-start.7 = (bf16[2,352,384]{2,1,0:T(8,128)(2,1)}, bf16[2,352,384]{2,1,0:T(8,128)(2,1)S(1)}, u32[]{:S(2)}) copy-start(bf16[2,352,384]{2,1,0:T(8,128)(2,1)S(1)} %collective-permute-done.9.refs_11_) | copy-start | bytes 1622020
  88.9 22.3 %collective-permute-start.17 = (bf16[2,352,384]{2,1,0:T(8,128)(2,1)S(1)}, bf16[2,352,384]{2,1,0:T(8,128)(2,1)S(1)}, u32[]{:S(2)}, u32[]{:S(2)}) collective-permute-start(bf16[2,352,384]{2,1,0:T(8,128)(2,1)S(1)} %pad_maximum_fusion.1.refs_0_), channel_id=1, source_target_pairs={{256,0},{257,1},{258,2},{259,3},{260,4},{261,5},{262,6},{263,7},{2... | collective-permute-start | bytes 1622024 | tf_op jit(solution)/shard_map/ppermute | solution.py:48
  98.6 68.7 %copy-start.11 = (bf16[2,352,384]{2,1,0:T(8,128)(2,1)}, bf16[2,352,384]{2,1,0:T(8,128)(2,1)S(1)}, u32[]{:S(2)}) copy-start(bf16[2,352,384]{2,1,0:T(8,128)(2,1)S(1)} %collective-permute-done.10.refs_12_) | copy-start | bytes 1622020
  98.6 24.3 %collective-permute-start.18 = (bf16[2,352,384]{2,1,0:T(8,128)(2,1)S(1)}, bf16[2,352,384]{2,1,0:T(8,128)(2,1)S(1)}, u32[]{:S(2)}, u32[]{:S(2)}) collective-permute-start(bf16[2,352,384]{2,1,0:T(8,128)(2,1)S(1)} %pad_maximum_fusion.1.refs_0_), channel_id=1, source_target_pairs={{384,0},{385,1},{386,2},{387,3},{388,4},{389,5},{390,6},{391,7},{3... | collective-permute-start | bytes 1622024 | tf_op jit(solution)/shard_map/ppermute | solution.py:48
  104.6 85.2 %copy-start.8 = (bf16[2,352,384]{2,1,0:T(8,128)(2,1)}, bf16[2,352,384]{2,1,0:T(8,128)(2,1)S(1)}, u32[]{:S(2)}) copy-start(bf16[2,352,384]{2,1,0:T(8,128)(2,1)S(1)} %collective-permute-done.16.refs_1_) | copy-start | bytes 1622020
  104.6 34.1 %collective-permute-start.11 = (bf16[2,352,384]{2,1,0:T(8,128)(2,1)S(1)}, bf16[2,352,384]{2,1,0:T(8,128)(2,1)S(1)}, u32[]{:S(2)}, u32[]{:S(2)}) collective-permute-start(bf16[2,352,384]{2,1,0:T(8,128)(2,1)S(1)} %collective-permute-done.7.refs_9_), channel_id=1, source_target_pairs={{32,0},{33,1},{34,2},{35,3},{36,4},{37,5},{38,6},{39,7},{40,8},{41... | collective-permute-start | bytes 1622024 | tf_op jit(solution)/shard_map/ppermute | solution.py:48
  111.2 78.6 %copy-start.9 = (bf16[2,352,384]{2,1,0:T(8,128)(2,1)}, bf16[2,352,384]{2,1,0:T(8,128)(2,1)S(1)}, u32[]{:S(2)}) copy-start(bf16[2,352,384]{2,1,0:T(8,128)(2,1)S(1)} %collective-permute-done.17.refs_2_) | copy-start | bytes 1622020
  111.2 29.9 %collective-permute-start.12 = (bf16[2,352,384]{2,1,0:T(8,128)(2,1)S(1)}, bf16[2,352,384]{2,1,0:T(8,128)(2,1)S(1)}, u32[]{:S(2)}, u32[]{:S(2)}) collective-permute-start(bf16[2,352,384]{2,1,0:T(8,128)(2,1)S(1)} %collective-permute-done.8.refs_10_), channel_id=1, source_target_pairs={{32,0},{33,1},{34,2},{35,3},{36,4},{37,5},{38,6},{39,7},{40,8},{41... | collective-permute-start | bytes 1622024 | tf_op jit(solution)/shard_map/ppermute | solution.py:48
  122.9 66.9 %copy-start.10 = (bf16[2,352,384]{2,1,0:T(8,128)(2,1)}, bf16[2,352,384]{2,1,0:T(8,128)(2,1)S(1)}, u32[]{:S(2)}) copy-start(bf16[2,352,384]{2,1,0:T(8,128)(2,1)S(1)} %collective-permute-done.18.refs_3_) | copy-start | bytes 1622020
  122.9 67.0 %collective-permute-start.19 = (bf16[2,352,384]{2,1,0:T(8,128)(2,1)S(1)}, bf16[2,352,384]{2,1,0:T(8,128)(2,1)S(1)}, u32[]{:S(2)}, u32[]{:S(2)}) collective-permute-start(bf16[2,352,384]{2,1,0:T(8,128)(2,1)S(1)} %pad_maximum_fusion.1.refs_0_), channel_id=1, source_target_pairs={{32,0},{33,1},{34,2},{35,3},{36,4},{37,5},{38,6},{39,7},{40,8},{41... | collective-permute-start | bytes 1622024 | tf_op jit(solution)/shard_map/ppermute | solution.py:48
  134.3 19.6 %copy-start.2 = (bf16[784,704]{1,0:T(8,128)(2,1)}, bf16[784,704]{1,0:T(8,128)(2,1)S(1)}, u32[]{:S(2)}) copy-start(bf16[784,704]{1,0:T(8,128)(2,1)S(1)} %collective-permute-done.refs_2_) | copy-start | bytes 3311620
  134.3 32.9 %collective-permute-start.13 = (bf16[2,352,384]{2,1,0:T(8,128)(2,1)S(1)}, bf16[2,352,384]{2,1,0:T(8,128)(2,1)}, u32[]{:S(2)}, u32[]{:S(2)}) collective-permute-start(bf16[2,352,384]{2,1,0:T(8,128)(2,1)S(1)} %collective-permute-done.9.refs_11_), channel_id=1, source_target_pairs={{32,0},{33,1},{34,2},{35,3},{36,4},{37,5},{38,6},{39,7},{40,8},{41... | collective-permute-start | bytes 1622024 | tf_op jit(solution)/shard_map/ppermute | solution.py:48
  136.7 30.5 %copy-start.3 = (bf16[784,704]{1,0:T(8,128)(2,1)}, bf16[784,704]{1,0:T(8,128)(2,1)S(1)}, u32[]{:S(2)}) copy-start(bf16[784,704]{1,0:T(8,128)(2,1)S(1)} %collective-permute-done.1.refs_3_) | copy-start | bytes 3311620
  136.7 53.1 %collective-permute-start.20 = (bf16[2,352,384]{2,1,0:T(8,128)(2,1)S(1)}, bf16[2,352,384]{2,1,0:T(8,128)(2,1)}, u32[]{:S(2)}, u32[]{:S(2)}) collective-permute-start(bf16[2,352,384]{2,1,0:T(8,128)(2,1)S(1)} %collective-permute-done.16.refs_1_), channel_id=1, source_target_pairs={{32,0},{33,1},{34,2},{35,3},{36,4},{37,5},{38,6},{39,7},{40,8},{41... | collective-permute-start | bytes 1622024 | tf_op jit(solution)/shard_map/ppermute | solution.py:48
  138.7 28.5 %copy-start.13 = (bf16[2,352,384]{2,1,0:T(8,128)(2,1)}, bf16[2,352,384]{2,1,0:T(8,128)(2,1)S(1)}, u32[]{:S(2)}) copy-start(bf16[2,352,384]{2,1,0:T(8,128)(2,1)S(1)} %collective-permute-done.11.refs_13_) | copy-start | bytes 1622020
  138.7 51.2 %collective-permute-start.21 = (bf16[2,352,384]{2,1,0:T(8,128)(2,1)S(1)}, bf16[2,352,384]{2,1,0:T(8,128)(2,1)}, u32[]{:S(2)}, u32[]{:S(2)}) collective-permute-start(bf16[2,352,384]{2,1,0:T(8,128)(2,1)S(1)} %collective-permute-done.17.refs_2_), channel_id=1, source_target_pairs={{32,0},{33,1},{34,2},{35,3},{36,4},{37,5},{38,6},{39,7},{40,8},{41... | collective-permute-start | bytes 1622024 | tf_op jit(solution)/shard_map/ppermute | solution.py:48
  141.1 0.8 copy-start.14
  141.9 48.0 %collective-permute-start.22 = (bf16[2,352,384]{2,1,0:T(8,128)(2,1)S(1)}, bf16[2,352,384]{2,1,0:T(8,128)(2,1)}, u32[]{:S(2)}, u32[]{:S(2)}) collective-permute-start(bf16[2,352,384]{2,1,0:T(8,128)(2,1)S(1)} %collective-permute-done.18.refs_3_), channel_id=1, source_target_pairs={{32,0},{33,1},{34,2},{35,3},{36,4},{37,5},{38,6},{39,7},{40,8},{41... | collective-permute-start | bytes 1622024 | tf_op jit(solution)/shard_map/ppermute | solution.py:48
  153.9 9.7 %copy-start.18 = (f32[2816]{0:T(1024)S(1)}, f32[2816]{0:T(1024)}, u32[]{:S(2)}) copy-start(f32[2816]{0:T(1024)} %param.21) | copy-start | bytes 33796
  153.9 10.3 %copy-start.22 = (f32[704]{0:T(1024)S(1)}, f32[704]{0:T(1024)}, u32[]{:S(2)}) copy-start(f32[704]{0:T(1024)} %param.18) | copy-start | bytes 8452
  154.0 10.8 %copy-start.23 = (f32[704]{0:T(1024)S(1)}, f32[704]{0:T(1024)}, u32[]{:S(2)}) copy-start(f32[704]{0:T(1024)} %param.19) | copy-start | bytes 8452
  154.0 11.4 %copy-start.19 = (f32[2816]{0:T(1024)S(1)}, f32[2816]{0:T(1024)}, u32[]{:S(2)}) copy-start(f32[2816]{0:T(1024)} %param.22) | copy-start | bytes 33796
  154.0 12.0 %copy-start.20 = (f32[2816]{0:T(1024)S(1)}, f32[2816]{0:T(1024)}, u32[]{:S(2)}) copy-start(f32[2816]{0:T(1024)} %param.23) | copy-start | bytes 33796
  154.0 12.6 %copy-start.24 = (f32[704]{0:T(1024)S(1)}, f32[704]{0:T(1024)}, u32[]{:S(2)}) copy-start(f32[704]{0:T(1024)} %param.25) | copy-start | bytes 8452
  189.8 0.8 copy-start.12

commit v2 on v1

v2 whole, which is shorter than its diff:
```python
import jax
import jax.numpy as jnp
from jax import lax
from jax.experimental import pallas as pl
from jax.experimental.pallas import tpu as pltpu
from jax.sharding import PartitionSpec as P

C, HID, H, W = 704, 2816, 28, 28
PIX = H * W
LANES = 128
CHUNKS = 6
SHARD = 88
MIB = 1024 * 1024
OFFSETS = ((0, 1, 7, 2), (4, 5, 3, 6))

vmem_spec = pl.BlockSpec(memory_space=pltpu.VMEM)
smem_spec = pl.BlockSpec(memory_space=pltpu.SMEM)
hbm_spec = pl.BlockSpec(memory_space=pl.ANY)


def after(value, *first):
    return lax.optimization_barrier((value,) + first)[0]


def place():
    v = lax.axis_index("video")
    t = lax.axis_index("tm")
    return v // 4, v % 2, t // 4, t % 4


def pick(table, index):
    value = jnp.int32(table[0])
    for k in range(1, len(table)):
        value = jnp.where(index == k, jnp.int32(table[k]), value)
    return value


def permute(value, source_of):
    pairs = []
    for x in range(4):
        for zh in range(2):
            for c in range(2):
                for y in range(8):
                    for zl in range(4):
                        src = source_of(x, zh, c, y, zl)
                        if src is None:
                            continue
                        pairs.append((flat(*src), flat(x, zh, c, y, zl)))
    return lax.ppermute(value, ("video", "tm"), pairs)


def flat(x, zh, c, y, zl):
    return ((x * 2 + zh) * 2 + c) * 32 + y * 4 + zl


def from_frame(by):
    def source_of(x, zh, c, y, zl):
        t = y * 4 + zl + by
        return (x, zh, c, t // 4, t % 4) if 0 <= t < 32 else None

    return source_of


def widen(value):
    if value.shape[-1] == LANES:
        return value
    zeros = jnp.zeros(value.shape[:-1] + (LANES - value.shape[-1],), value.dtype)
    return jnp.concatenate([value, zeros], axis=-1)


def lanes(chunk):
    return slice(chunk * LANES, min((chunk + 1) * LANES, C))


def flatten_kernel(clip_ref, x_ref, flat_ref, masked_ref):
    keep = (1 - clip_ref[0]).astype(jnp.float32)
    for g in range(7):
        rows = jnp.concatenate([x_ref[4 * g + r].astype(jnp.float32) for r in range(4)], axis=0)
        flat_ref[112 * g : 112 * (g + 1), :] = rows.astype(jnp.bfloat16)
        masked_ref[112 * g : 112 * (g + 1), :] = (rows * keep).astype(jnp.bfloat16)


def flatten(clip, frame):
    out = jax.ShapeDtypeStruct((PIX, C), jnp.bfloat16)
    return pl.pallas_call(
        flatten_kernel,
        out_shape=(out, out),
        in_specs=[smem_spec, vmem_spec],
        out_specs=(vmem_spec, vmem_spec),
        compiler_params=pltpu.CompilerParams(vmem_limit_bytes=8 * MIB),
        name="flatten",
    )(clip, frame)


def conv_kernel(first, count, x_ref, k_ref, t_ref, b_ref, o_ref, xp, kb, bb):
    xp[...] = jnp.zeros_like(xp)
    for n in range(count):
        part = lanes(first + n)
        for i in range(H):
            xp[n, 3 + i, 3:31, :] = widen(x_ref[i, :, part].astype(jnp.float32))
        for tap in range(49):
            row = widen(k_ref[tap : tap + 1, part])
            if tap == 24:
                row = row + widen(t_ref[1:2, part])
            kb[n, tap] = jnp.broadcast_to(row, (8, LANES))
        bb[n] = jnp.broadcast_to(widen(b_ref[part][None]), (8, LANES))

    def body(step, carry):
        n = step // 7
        g = step % 7
        done = [[None] * 4 for _ in range(4)]
        for jb in range(4):
            acc = [bb[n]] * 4
            for b in range(7):
                xs = [xp[n, 4 * g + q, 8 * jb + b : 8 * jb + b + 8, :] for q in range(10)]
                for a in range(7):
                    kv = kb[n, 7 * a + b]
                    for r in range(4):
                        acc[r] = acc[r] + kv * xs[r + a]
            for r in range(4):
                done[r][jb] = acc[r] if jb < 3 else acc[r][:4]
        rows = jnp.concatenate([done[r][jb] for r in range(4) for jb in range(4)], axis=0)
        o_ref[n, pl.ds(pl.multiple_of(112 * g, 8), 112), :] = rows
        return carry

    lax.fori_loop(0, 7 * count, body, 0)


def conv(first, count, frame, space_kernel, time_kernel, conv_bias):
    return pl.pallas_call(
        lambda *refs: conv_kernel(first, count, *refs),
        out_shape=jax.ShapeDtypeStruct((count, PIX, LANES), jnp.float32),
        in_specs=[vmem_spec] * 4,
        out_specs=vmem_spec,
        scratch_shapes=[
            pltpu.VMEM((count, 34, 40, LANES), jnp.float32),
            pltpu.VMEM((count, 49, 8, LANES), jnp.float32),
            pltpu.VMEM((count, 8, LANES), jnp.float32),
        ],
        compiler_params=pltpu.CompilerParams(vmem_limit_bytes=14 * MIB),
        name="conv",
    )(frame, space_kernel, time_kernel, conv_bias)


def join_kernel(*refs):
    for k, source in enumerate(refs[:-1]):
        refs[-1][k] = source[...]


def join(blocks):
    shape = (len(blocks),) + blocks[0].shape
    return pl.pallas_call(
        join_kernel,
        out_shape=jax.ShapeDtypeStruct(shape, jnp.bfloat16),
        in_specs=[vmem_spec] * len(blocks),
        out_specs=vmem_spec,
        compiler_params=pltpu.CompilerParams(vmem_limit_bytes=12 * MIB),
        name="join",
    )(*blocks)


def split_kernel(*refs):
    for r in range(4):
        refs[4][r] = refs[r][0]
        refs[5][r] = refs[r][1]


def split(blocks):
    out = jax.ShapeDtypeStruct((4, SHARD, C), jnp.bfloat16)
    return pl.pallas_call(
        split_kernel,
        out_shape=(out, out),
        in_specs=[vmem_spec] * 4,
        out_specs=(vmem_spec, vmem_spec),
        compiler_params=pltpu.CompilerParams(vmem_limit_bytes=12 * MIB),
        name="split",
    )(*blocks)


def place_blocks(own, other, weight):
    x, core, y, zl = place()
    for step in range(4):
        for side, ref in ((core, own), (1 - core, other)):
            for r in range(4):
                column = (x + step + r) % 4
                offset = jnp.where(side == 0, pick(OFFSETS[0], column), pick(OFFSETS[1], column))
                row = (((y + offset) % 8) * 4 + (zl ^ r)) * SHARD
                weight[pl.ds(pl.multiple_of(row, 8), SHARD), :] = ref[step, r].astype(jnp.float32)


def up_kernel(clip_ref, *refs):
    (c0_ref, c1_ref, prev_ref, next_ref, t_ref, gain_ref, nbias_ref, ubias_ref) = refs[:8]
    own, other, hid_ref, energy_ref, weight, normed = refs[8:]
    place_blocks(own, other, weight)
    keep = (1 - clip_ref[0]).astype(jnp.float32)

    gain = [widen(gain_ref[lanes(n)][None]) for n in range(CHUNKS)]
    nbias = [widen(nbias_ref[lanes(n)][None]) for n in range(CHUNKS)]

    def norm_rows(step, carry):
        rows = pl.ds(pl.multiple_of(step * 112, 16), 112)
        parts = []
        for n in range(CHUNKS):
            part = lanes(n)
            base = c0_ref[n, rows, :] if n < 3 else c1_ref[n - 3, rows, :]
            before = widen(prev_ref[rows, part].astype(jnp.float32)) * (widen(t_ref[0:1, part]) * keep)
            after = widen(next_ref[rows, part].astype(jnp.float32)) * widen(t_ref[2:3, part])
            parts.append(base + before + after)
        total = parts[0]
        for n in range(1, CHUNKS):
            total = total + parts[n]
        mean = jnp.sum(total, axis=-1, keepdims=True) * (1.0 / C)
        parts = [p - mean for p in parts]
        lane = lax.broadcasted_iota(jnp.int32, parts[-1].shape, 1)
        parts[-1] = jnp.where(lane < C - 5 * LANES, parts[-1], 0.0)
        total = parts[0] * parts[0]
        for n in range(1, CHUNKS):
            total = total + parts[n] * parts[n]
        var = jnp.sum(total, axis=-1, keepdims=True) * (1.0 / C)
        scale = lax.rsqrt(var + 1e-06)
        for n in range(CHUNKS):
            value = parts[n] * scale * gain[n] + nbias[n]
            normed[rows, n * LANES : (n + 1) * LANES] = value.astype(jnp.bfloat16)
        return carry

    lax.fori_loop(0, PIX // 112, norm_rows, 0)

    def units(step, carry):
        cols = pl.ds(pl.multiple_of(step * 256, 256), 256)
        dims = (((1,), (1,)), ((), ()))
        value = lax.dot_general(
            normed[:, :C], weight[cols, :].astype(jnp.bfloat16), dims, preferred_element_type=jnp.float32
        )
        value = value + ubias_ref[cols][None]
        hid = (0.5 * value * (1.0 + lax.erf(value * 0.7071067811865476))).astype(jnp.bfloat16)
        hid_ref[:, cols] = hid
        wide = hid.astype(jnp.float32)
        energy_ref[:, cols] = jnp.sum(wide * wide, axis=0, keepdims=True)
        return carry

    lax.fori_loop(0, HID // 256, units, 0)


def up(clip, conv0, conv1, prev, nxt, time_kernel, gain, nbias, ubias, own, other):
    return pl.pallas_call(
        up_kernel,
        out_shape=(
            jax.ShapeDtypeStruct((PIX, HID), jnp.bfloat16),
            jax.ShapeDtypeStruct((1, HID), jnp.float32),
        ),
        in_specs=[smem_spec] + [vmem_spec] * 8 + [vmem_spec] * 2,
        out_specs=(vmem_spec, vmem_spec),
        scratch_shapes=[
            pltpu.VMEM((HID, C), jnp.float32),
            pltpu.VMEM((PIX, CHUNKS * LANES), jnp.bfloat16),
        ],
        compiler_params=pltpu.CompilerParams(vmem_limit_bytes=29 * MIB),
        name="up",
    )(clip, conv0, conv1, prev, nxt, time_kernel, gain, nbias, ubias, own, other)


def down_kernel(hid_ref, energy_ref, gamma_ref, beta_ref, dbias_ref, flat_ref, *refs):
    own, other, out_ref, weight, grn, sums = refs
    place_blocks(own, other, weight)
    energy = jnp.sqrt(energy_ref[...])
    ratio = energy / (jnp.sum(energy, axis=1, keepdims=True) * (1.0 / HID) + 1e-06)
    grow = gamma_ref[...][None] * ratio + 1.0
    beta = beta_ref[...][None]

    def scale(step, carry):
        rows = pl.ds(pl.multiple_of(step * 16, 16), 16)
        grn[rows, :] = (hid_ref[rows, :].astype(jnp.float32) * grow + beta).astype(jnp.bfloat16)
        return carry

    lax.fori_loop(0, PIX // 16, scale, 0)
    for cols in (slice(0, 256), slice(256, 512), slice(512, C)):
        sums[:, cols] = jnp.dot(grn[...], weight[:, cols].astype(jnp.bfloat16), preferred_element_type=jnp.float32)
    for g in range(7):
        rows = slice(112 * g, 112 * (g + 1))
        value = sums[rows, :] + dbias_ref[...][None] + flat_ref[rows, :].astype(jnp.float32)
        for r in range(4):
            out_ref[4 * g + r] = value[28 * r : 28 * (r + 1)].astype(jnp.bfloat16)


def down(hid, energy, gamma, beta, dbias, flat_frame, own, other):
    return pl.pallas_call(
        down_kernel,
        out_shape=jax.ShapeDtypeStruct((H, W, C), jnp.bfloat16),
        in_specs=[vmem_spec] * 6 + [vmem_spec] * 2,
        out_specs=vmem_spec,
        scratch_shapes=[
            pltpu.VMEM((HID, C), jnp.float32),
            pltpu.VMEM((PIX, HID), jnp.bfloat16),
            pltpu.VMEM((PIX, C), jnp.float32),
        ],
        compiler_params=pltpu.CompilerParams(vmem_limit_bytes=33 * MIB),
        name="down",
    )(hid, energy, gamma, beta, dbias, flat_frame, own, other)


def spread_yz(both):
    blocks = []
    for r in range(4):
        blocks.append(
            permute(
                both,
                lambda x, zh, c, y, zl: (x, zh, c, (y + OFFSETS[c][(x + r) % 4]) % 8, zl ^ r),
            )
        )
    return blocks


def from_x(block, by):
    return permute(block, lambda x, zh, c, y, zl: ((x + by) % 4, zh, c, y, zl))


def swap_core(block):
    return permute(block, lambda x, zh, c, y, zl: (x, zh, 1 - c, y, zl))


def per_device(
    frames,
    clip_cut,
    space_kernel,
    time_kernel,
    conv_bias,
    norm_gain,
    norm_bias,
    up_weight,
    up_bias,
    grn_gamma,
    grn_beta,
    down_weight,
    down_bias,
):
    frame = frames[0]
    both = jnp.stack([up_weight.T, down_weight])
    blocks = spread_yz(both)
    conv0 = conv(0, 3, frame, space_kernel, time_kernel, conv_bias)
    flat_frame, masked = flatten(clip_cut, frame)
    blocks = [after(block, flat_frame, conv0) for block in blocks]
    prev = permute(after(flat_frame, *blocks), from_frame(-1))
    nxt = permute(after(masked, *blocks), from_frame(1))
    up_yz, down_yz = split(blocks)
    conv1 = conv(3, 3, frame, space_kernel, time_kernel, after(conv_bias, up_yz))
    up_1 = from_x(up_yz, 1)
    up_3 = from_x(up_yz, 3)
    down_3 = from_x(down_yz, 3)
    down_1 = from_x(after(down_yz, conv1, up_1), 1)
    up_2 = from_x(after(up_1, conv1), 1)
    down_2 = from_x(after(down_3, up_3), 3)
    up_own = join([after(block, prev) for block in (up_yz, up_1, up_2, up_3)])
    up_other = swap_core(up_own)
    down_own = join([after(block, nxt) for block in (down_yz, down_1, down_2, down_3)])
    down_other = swap_core(down_own)
    hid, energy = up(
        clip_cut,
        conv0,
        conv1,
        prev,
        nxt,
        time_kernel,
        norm_gain,
        norm_bias,
        up_bias,
        up_own,
        up_other,
    )
    out = down(
        hid, energy, grn_gamma, grn_beta, down_bias, flat_frame, down_own, down_other
    )
    return out[None]


def solution(mesh):
    return jax.shard_map(
        per_device,
        mesh=mesh,
        in_specs=(
            P(("video", "tm"), None, None, None),
            P(("video", "tm")),
            P(),
            P(),
            P(),
            P(),
            P(),
            P(None, "tm"),
            P(),
            P(),
            P(),
            P("tm", None),
            P(),
        ),
        out_specs=P(("video", "tm"), None, None, None),
        check_vma=False,
    )
```

time: 202 us -> 121 us (0.60)
  the two profiles are of different devices: /device:TPU:73 before, /device:TPU:9 now
where the time goes in v2:
time: 121 us
  starting transfers between devices  54.8 us (45%)
  Pallas kernels  31 us (26%)
  waiting for transfers between devices  30.7 us (25%)
  local copies, waits for them, and re-layouts  2.35 us (2%)
    ppermute x14, starting transfers between devices, permute(): return lax.ppermute(value, ('video', 'tm'), pairs)  54.8 us
    ppermute x14, waiting for transfers between devices, permute(): return lax.ppermute(value, ('video', 'tm'), pairs)  30.7 us
    pallas_call x2, Pallas kernels, conv(): pl.pallas_call(lambda *refs: conv_kernel(first, count, *refs), out_shape=...  14.1 us
    pallas_call x1, Pallas kernels, up(): pl.pallas_call(up_kernel, out_shape=(jax.ShapeDtypeStruct((PIX, HID), jnp...  9.15 us
    pallas_call x1, Pallas kernels, down(): pl.pallas_call(down_kernel, out_shape=jax.ShapeDtypeStruct((H, W, C), jnp...  7.07 us
  transfers between devices with their start and end apart: 14, of which 6 were waited for; matrix products, arithmetic and copies ran while one was open for 0% of the time, Pallas kernels for 20%

profile of v2, /device:TPU:9, one launch (start us, length us, event | category | flops | bytes accessed | tf_op | source)
XLA Modules:
  0.0 120.9 jit_solution(13715718406879615798)
XLA Ops:
  0.0 1.0 pad_maximum_fusion
  1.1 6.6 %collective-permute-start = (bf16[2,88,704]{2,1,0:T(8,128)(2,1)S(1)}, bf16[2,88,704]{2,1,0:T(8,128)(2,1)S(1)}, u32[]{:S(2)}, u32[]{:S(2)}) collective-permute-start(bf16[2,88,704]{2,1,0:T(8,128)(2,1)S(1)} %pad_maximum_fusion), channel_id=1, source_target_pairs={{0,0},{1,1},{2,2},{3,3},{4,4},{5,5},{6,6},{7,7},{8,8},{9,9},{10,10... | collective-permute-start | bytes 743432 | tf_op jit(solution)/shard_map/ppermute | solution.py:49
  7.6 3.6 %collective-permute-start.1 = (bf16[2,88,704]{2,1,0:T(8,128)(2,1)S(1)}, bf16[2,88,704]{2,1,0:T(8,128)(2,1)S(1)}, u32[]{:S(2)}, u32[]{:S(2)}) collective-permute-start(bf16[2,88,704]{2,1,0:T(8,128)(2,1)S(1)} %pad_maximum_fusion), channel_id=1, source_target_pairs={{5,0},{4,1},{7,2},{6,3},{9,4},{8,5},{11,6},{10,7},{13,8},{12,9},{1... | collective-permute-start | bytes 743432 | tf_op jit(solution)/shard_map/ppermute | solution.py:49
  11.2 10.1 %collective-permute-start.2 = (bf16[2,88,704]{2,1,0:T(8,128)(2,1)S(1)}, bf16[2,88,704]{2,1,0:T(8,128)(2,1)S(1)}, u32[]{:S(2)}, u32[]{:S(2)}) collective-permute-start(bf16[2,88,704]{2,1,0:T(8,128)(2,1)S(1)} %pad_maximum_fusion), channel_id=1, source_target_pairs={{30,0},{31,1},{28,2},{29,3},{2,4},{3,5},{0,6},{1,7},{6,8},{7,9},{4... | collective-permute-start | bytes 743432 | tf_op jit(solution)/shard_map/ppermute | solution.py:49
  21.3 1.9 %collective-permute-start.3 = (bf16[2,88,704]{2,1,0:T(8,128)(2,1)S(1)}, bf16[2,88,704]{2,1,0:T(8,128)(2,1)S(1)}, u32[]{:S(2)}, u32[]{:S(2)}) collective-permute-start(bf16[2,88,704]{2,1,0:T(8,128)(2,1)S(1)} %pad_maximum_fusion), channel_id=1, source_target_pairs={{11,0},{10,1},{9,2},{8,3},{15,4},{14,5},{13,6},{12,7},{19,8},{18,9... | collective-permute-start | bytes 743432 | tf_op jit(solution)/shard_map/ppermute | solution.py:49
  23.9 0.0 copy-start
  23.9 1.3 %copy-done = bf16[1,28,28,704]{3,2,1,0:T(8,128)(2,1)S(1)} copy-done((bf16[1,28,28,704]{3,2,1,0:T(8,128)(2,1)S(1)}, bf16[1,28,28,704]{3,2,1,0:T(8,128)(2,1)}, u32[]{:S(2)}) %copy-start) | copy-done | bytes 1103896
  25.3 0.3 flatten.1
  25.6 1.0 copy-done.1
  26.6 7.0 %conv.2.refs_0_ = f32[3,784,128]{2,1,0:T(8,128)S(1)} custom-call(bf16[28,28,704]{2,1,0:T(8,128)(2,1)S(1)} %bitcast.7, f32[49,704]{1,0:T(8,128)S(1)} %copy-done.2, f32[3,704]{1,0:T(4,128)S(1)} %copy-done.3, f32[704]{0:T(1024)S(1)} %copy-done.4), custom_call_target="tpu_custom_call" | custom-call | tf_op jit(solution)/shard_map/conv/pallas_call | solution.py:130
  33.6 0.0 collective-permute-done.refs_0_
  33.6 0.0 collective-permute-done.1.refs_1_
  33.6 0.3 collective-permute-done.2.refs_2_
  33.9 8.6 %collective-permute-done.3.refs_3_ = bf16[2,88,704]{2,1,0:T(8,128)(2,1)S(1)} collective-permute-done((bf16[2,88,704]{2,1,0:T(8,128)(2,1)S(1)}, bf16[2,88,704]{2,1,0:T(8,128)(2,1)S(1)}, u32[]{:S(2)}, u32[]{:S(2)}) %collective-permute-start.3) | collective-permute-done | bytes 247840 | tf_op jit(solution)/shard_map/ppermute | solution.py:49
  42.5 1.9 %collective-permute-start.4 = (bf16[784,704]{1,0:T(8,128)(2,1)S(1)}, bf16[784,704]{1,0:T(8,128)(2,1)S(1)}, u32[]{:S(2)}, u32[]{:S(2)}) collective-permute-start(bf16[784,704]{1,0:T(8,128)(2,1)S(1)} %get-tuple-element.36.flat_ref), channel_id=1, source_target_pairs={{0,1},{1,2},{2,3},{3,4},{4,5},{5,6},{6,7},{7,8},{8,9},{9,10},{10,1... | collective-permute-start | bytes 3311624 | tf_op jit(solution)/shard_map/ppermute | solution.py:49
  44.4 6.1 %collective-permute-start.5 = (bf16[784,704]{1,0:T(8,128)(2,1)S(1)}, bf16[784,704]{1,0:T(8,128)(2,1)S(1)}, u32[]{:S(2)}, u32[]{:S(2)}) collective-permute-start(bf16[784,704]{1,0:T(8,128)(2,1)S(1)} %get-tuple-element.38), channel_id=1, source_target_pairs={{1,0},{2,1},{3,2},{4,3},{5,4},{6,5},{7,6},{8,7},{9,8},{10,9},{11,1... | collective-permute-start | bytes 3311624 | tf_op jit(solution)/shard_map/ppermute | solution.py:49
  50.4 0.1 split.1
  50.5 5.2 %collective-permute-start.6 = (bf16[4,88,704]{2,1,0:T(8,128)(2,1)S(1)}, bf16[4,88,704]{2,1,0:T(8,128)(2,1)S(1)}, u32[]{:S(2)}, u32[]{:S(2)}) collective-permute-start(bf16[4,88,704]{2,1,0:T(8,128)(2,1)S(1)} %get-tuple-element.39.refs_0_), channel_id=1, source_target_pairs={{128,0},{129,1},{130,2},{131,3},{132,4},{133,5},{134,6},{135,7},{1... | collective-permute-start | bytes 1486856 | tf_op jit(solution)/shard_map/ppermute | solution.py:49
  55.7 1.9 %collective-permute-start.8 = (bf16[4,88,704]{2,1,0:T(8,128)(2,1)S(1)}, bf16[4,88,704]{2,1,0:T(8,128)(2,1)S(1)}, u32[]{:S(2)}, u32[]{:S(2)}) collective-permute-start(bf16[4,88,704]{2,1,0:T(8,128)(2,1)S(1)} %get-tuple-element.39.refs_0_), channel_id=1, source_target_pairs={{384,0},{385,1},{386,2},{387,3},{388,4},{389,5},{390,6},{391,7},{3... | collective-permute-start | bytes 1486856 | tf_op jit(solution)/shard_map/ppermute | solution.py:49
  57.6 1.9 %collective-permute-start.11 = (bf16[4,88,704]{2,1,0:T(8,128)(2,1)S(1)}, bf16[4,88,704]{2,1,0:T(8,128)(2,1)S(1)}, u32[]{:S(2)}, u32[]{:S(2)}) collective-permute-start(bf16[4,88,704]{2,1,0:T(8,128)(2,1)S(1)} %get-tuple-element.48.refs_0_), channel_id=1, source_target_pairs={{384,0},{385,1},{386,2},{387,3},{388,4},{389,5},{390,6},{391,7},{3... | collective-permute-start | bytes 1486856 | tf_op jit(solution)/shard_map/ppermute | solution.py:49
  59.6 7.0 %conv.3.refs_1_ = f32[3,784,128]{2,1,0:T(8,128)S(1)} custom-call(bf16[28,28,704]{2,1,0:T(8,128)(2,1)S(1)} %bitcast.8, f32[49,704]{1,0:T(8,128)S(1)} %copy-done.2, f32[3,704]{1,0:T(4,128)S(1)} %copy-done.3, f32[704]{0:T(1024)S(1)} %copy-done.4), custom_call_target="tpu_custom_call" | custom-call | tf_op jit(solution)/shard_map/conv/pallas_call | solution.py:130
  66.6 0.0 collective-permute-done.6.refs_1_
  66.6 4.6 %collective-permute-start.7 = (bf16[4,88,704]{2,1,0:T(8,128)(2,1)S(1)}, bf16[4,88,704]{2,1,0:T(8,128)(2,1)S(1)}, u32[]{:S(2)}, u32[]{:S(2)}) collective-permute-start(bf16[4,88,704]{2,1,0:T(8,128)(2,1)S(1)} %collective-permute-done.6.refs_1_), channel_id=1, source_target_pairs={{128,0},{129,1},{130,2},{131,3},{132,4},{133,5},{134,6},{135,7},{1... | collective-permute-start | bytes 1486856 | tf_op jit(solution)/shard_map/ppermute | solution.py:49
  71.2 1.9 %collective-permute-done.8.refs_3_ = bf16[4,88,704]{2,1,0:T(8,128)(2,1)S(1)} collective-permute-done((bf16[4,88,704]{2,1,0:T(8,128)(2,1)S(1)}, bf16[4,88,704]{2,1,0:T(8,128)(2,1)S(1)}, u32[]{:S(2)}, u32[]{:S(2)}) %collective-permute-start.8) | collective-permute-done | bytes 495648 | tf_op jit(solution)/shard_map/ppermute | solution.py:49
  73.1 1.9 %collective-permute-start.10 = (bf16[4,88,704]{2,1,0:T(8,128)(2,1)S(1)}, bf16[4,88,704]{2,1,0:T(8,128)(2,1)S(1)}, u32[]{:S(2)}, u32[]{:S(2)}) collective-permute-start(bf16[4,88,704]{2,1,0:T(8,128)(2,1)S(1)} %get-tuple-element.48.refs_0_), channel_id=1, source_target_pairs={{128,0},{129,1},{130,2},{131,3},{132,4},{133,5},{134,6},{135,7},{1... | collective-permute-start | bytes 1486856 | tf_op jit(solution)/shard_map/ppermute | solution.py:49
  75.0 9.5 %collective-permute-done.11.refs_3_ = bf16[4,88,704]{2,1,0:T(8,128)(2,1)S(1)} collective-permute-done((bf16[4,88,704]{2,1,0:T(8,128)(2,1)S(1)}, bf16[4,88,704]{2,1,0:T(8,128)(2,1)S(1)}, u32[]{:S(2)}, u32[]{:S(2)}) %collective-permute-start.11) | collective-permute-done | bytes 495648 | tf_op jit(solution)/shard_map/ppermute | solution.py:49
  84.5 1.9 %collective-permute-start.12 = (bf16[4,88,704]{2,1,0:T(8,128)(2,1)S(1)}, bf16[4,88,704]{2,1,0:T(8,128)(2,1)S(1)}, u32[]{:S(2)}, u32[]{:S(2)}) collective-permute-start(bf16[4,88,704]{2,1,0:T(8,128)(2,1)S(1)} %collective-permute-done.11.refs_3_), channel_id=1, source_target_pairs={{384,0},{385,1},{386,2},{387,3},{388,4},{389,5},{390,6},{391,7},{3... | collective-permute-start | bytes 1486856 | tf_op jit(solution)/shard_map/ppermute | solution.py:49
  86.5 8.4 %collective-permute-done.4.refs_2_ = bf16[784,704]{1,0:T(8,128)(2,1)S(1)} collective-permute-done((bf16[784,704]{1,0:T(8,128)(2,1)S(1)}, bf16[784,704]{1,0:T(8,128)(2,1)S(1)}, u32[]{:S(2)}, u32[]{:S(2)}) %collective-permute-start.4) | collective-permute-done | bytes 1103904 | tf_op jit(solution)/shard_map/ppermute | solution.py:49
  94.9 0.0 collective-permute-done.7.refs_2_
  94.9 0.1 join.2.refs_8_
  95.0 0.0 copy-start.5
  95.1 0.0 copy-start.8
  95.1 0.0 copy-start.9
  95.1 4.0 %collective-permute-start.9 = (bf16[4,4,88,704]{3,2,1,0:T(8,128)(2,1)S(1)}, bf16[4,4,88,704]{3,2,1,0:T(8,128)(2,1)S(1)}, u32[]{:S(2)}, u32[]{:S(2)}) collective-permute-start(bf16[4,4,88,704]{3,2,1,0:T(8,128)(2,1)S(1)} %join.2.refs_8_), channel_id=1, source_target_pairs={{32,0},{33,1},{34,2},{35,3},{36,4},{37,5},{38,6},{39,7},{40,8},{41... | collective-permute-start | bytes 5947400 | tf_op jit(solution)/shard_map/ppermute | solution.py:49
  99.1 0.0 collective-permute-done.5.refs_3_
  99.1 0.0 collective-permute-done.10.refs_1_
  99.1 2.0 %collective-permute-done.12.refs_2_ = bf16[4,88,704]{2,1,0:T(8,128)(2,1)S(1)} collective-permute-done((bf16[4,88,704]{2,1,0:T(8,128)(2,1)S(1)}, bf16[4,88,704]{2,1,0:T(8,128)(2,1)S(1)}, u32[]{:S(2)}, u32[]{:S(2)}) %collective-permute-start.12) | collective-permute-done | bytes 495648 | tf_op jit(solution)/shard_map/ppermute | solution.py:49
  101.1 0.1 join.3.refs_0_
  101.2 0.0 copy-start.6
  101.3 0.0 copy-start.7
  101.3 0.0 copy-start.10
  101.3 3.3 %collective-permute-start.13 = (bf16[4,4,88,704]{3,2,1,0:T(8,128)(2,1)S(1)}, bf16[4,4,88,704]{3,2,1,0:T(8,128)(2,1)S(1)}, u32[]{:S(2)}, u32[]{:S(2)}) collective-permute-start(bf16[4,4,88,704]{3,2,1,0:T(8,128)(2,1)S(1)} %join.3.refs_0_), channel_id=1, source_target_pairs={{32,0},{33,1},{34,2},{35,3},{36,4},{37,5},{38,6},{39,7},{40,8},{41... | collective-permute-start | bytes 5947400 | tf_op jit(solution)/shard_map/ppermute | solution.py:49
  104.6 0.0 collective-permute-done.9.refs_9_
  104.6 0.0 copy-done.5
  104.6 0.0 copy-done.8
  104.6 9.2 %up.1 = (bf16[784,2816]{1,0:T(8,128)(2,1)S(1)}, f32[1,2816]{1,0:T(1,128)S(1)}) custom-call(s32[1]{0:T(128)S(6)} %copy.14.clip_ref, f32[3,784,128]{2,1,0:T(8,128)S(1)} %conv.2.refs_0_, f32[3,784,128]{2,1,0:T(8,128)S(1)} %conv.3.refs_1_, bf16[784,704]{1,0:T(8,128)(2,1)S(1)} %collective-permute-done.4.refs_2_, ...), custom_call_target="tpu_custom_call" | custom-call | tf_op jit(solution)/shard_map/up/pallas_call | solution.py:245
  113.8 0.0 collective-permute-done.13.refs_1_
  113.8 7.1 %down.1 = bf16[28,28,704]{2,1,0:T(8,128)(2,1)} custom-call(bf16[784,2816]{1,0:T(8,128)(2,1)S(1)} %get-tuple-element.44.hid_ref, f32[1,2816]{1,0:T(1,128)S(1)} %get-tuple-element.45.energy_ref, f32[2816]{0:T(1024)S(1)} %copy-done.6, f32[2816]{0:T(1024)S(1)} %copy-done.7, f32[704]{0:T(1024)S(1)} %copy-done.10, ...), custom_call_target="tpu_custom_call" | custom-call | tf_op jit(solution)/shard_map/down/pallas_call | solution.py:286
  (11 shorter events, 0.0 us)
Async XLA Ops:
  0.0 25.6 %copy-start.2 = (f32[49,704]{1,0:T(8,128)S(1)}, f32[49,704]{1,0:T(8,128)}, u32[]{:S(2)}) copy-start(f32[49,704]{1,0:T(8,128)} %refs_1_.3) | copy-start | bytes 413956
  0.0 25.6 %copy-start.3 = (f32[3,704]{1,0:T(4,128)S(1)}, f32[3,704]{1,0:T(4,128)}, u32[]{:S(2)}) copy-start(f32[3,704]{1,0:T(4,128)} %refs_4_.1) | copy-start | bytes 25348
  0.0 25.6 %copy-start.4 = (f32[704]{0:T(1024)S(1)}, f32[704]{0:T(1024)}, u32[]{:S(2)}) copy-start(f32[704]{0:T(1024)} %refs_3_.2) | copy-start | bytes 8452
  1.1 32.6 %collective-permute-start = (bf16[2,88,704]{2,1,0:T(8,128)(2,1)S(1)}, bf16[2,88,704]{2,1,0:T(8,128)(2,1)S(1)}, u32[]{:S(2)}, u32[]{:S(2)}) collective-permute-start(bf16[2,88,704]{2,1,0:T(8,128)(2,1)S(1)} %pad_maximum_fusion), channel_id=1, source_target_pairs={{0,0},{1,1},{2,2},{3,3},{4,4},{5,5},{6,6},{7,7},{8,8},{9,9},{10,10... | collective-permute-start | bytes 743432 | tf_op jit(solution)/shard_map/ppermute | solution.py:49
  7.6 26.0 %collective-permute-start.1 = (bf16[2,88,704]{2,1,0:T(8,128)(2,1)S(1)}, bf16[2,88,704]{2,1,0:T(8,128)(2,1)S(1)}, u32[]{:S(2)}, u32[]{:S(2)}) collective-permute-start(bf16[2,88,704]{2,1,0:T(8,128)(2,1)S(1)} %pad_maximum_fusion), channel_id=1, source_target_pairs={{5,0},{4,1},{7,2},{6,3},{9,4},{8,5},{11,6},{10,7},{13,8},{12,9},{1... | collective-permute-start | bytes 743432 | tf_op jit(solution)/shard_map/ppermute | solution.py:49
  11.2 22.7 %collective-permute-start.2 = (bf16[2,88,704]{2,1,0:T(8,128)(2,1)S(1)}, bf16[2,88,704]{2,1,0:T(8,128)(2,1)S(1)}, u32[]{:S(2)}, u32[]{:S(2)}) collective-permute-start(bf16[2,88,704]{2,1,0:T(8,128)(2,1)S(1)} %pad_maximum_fusion), channel_id=1, source_target_pairs={{30,0},{31,1},{28,2},{29,3},{2,4},{3,5},{0,6},{1,7},{6,8},{7,9},{4... | collective-permute-start | bytes 743432 | tf_op jit(solution)/shard_map/ppermute | solution.py:49
  21.3 21.1 %collective-permute-start.3 = (bf16[2,88,704]{2,1,0:T(8,128)(2,1)S(1)}, bf16[2,88,704]{2,1,0:T(8,128)(2,1)S(1)}, u32[]{:S(2)}, u32[]{:S(2)}) collective-permute-start(bf16[2,88,704]{2,1,0:T(8,128)(2,1)S(1)} %pad_maximum_fusion), channel_id=1, source_target_pairs={{11,0},{10,1},{9,2},{8,3},{15,4},{14,5},{13,6},{12,7},{19,8},{18,9... | collective-permute-start | bytes 743432 | tf_op jit(solution)/shard_map/ppermute | solution.py:49
  23.9 1.3 %copy-start = (bf16[1,28,28,704]{3,2,1,0:T(8,128)(2,1)S(1)}, bf16[1,28,28,704]{3,2,1,0:T(8,128)(2,1)}, u32[]{:S(2)}) copy-start(bf16[1,28,28,704]{3,2,1,0:T(8,128)(2,1)} %param.13) | copy-start | bytes 3311620
  25.3 1.3 %copy-start.1 = (bf16[1,28,28,704]{3,2,1,0:T(8,128)(2,1)S(1)}, bf16[1,28,28,704]{3,2,1,0:T(8,128)(2,1)}, u32[]{:S(2)}) copy-start(bf16[1,28,28,704]{3,2,1,0:T(8,128)(2,1)} %param.13) | copy-start | bytes 3311620
  42.5 52.4 %collective-permute-start.4 = (bf16[784,704]{1,0:T(8,128)(2,1)S(1)}, bf16[784,704]{1,0:T(8,128)(2,1)S(1)}, u32[]{:S(2)}, u32[]{:S(2)}) collective-permute-start(bf16[784,704]{1,0:T(8,128)(2,1)S(1)} %get-tuple-element.36.flat_ref), channel_id=1, source_target_pairs={{0,1},{1,2},{2,3},{3,4},{4,5},{5,6},{6,7},{7,8},{8,9},{9,10},{10,1... | collective-permute-start | bytes 3311624 | tf_op jit(solution)/shard_map/ppermute | solution.py:49
  44.4 54.7 %collective-permute-start.5 = (bf16[784,704]{1,0:T(8,128)(2,1)S(1)}, bf16[784,704]{1,0:T(8,128)(2,1)S(1)}, u32[]{:S(2)}, u32[]{:S(2)}) collective-permute-start(bf16[784,704]{1,0:T(8,128)(2,1)S(1)} %get-tuple-element.38), channel_id=1, source_target_pairs={{1,0},{2,1},{3,2},{4,3},{5,4},{6,5},{7,6},{8,7},{9,8},{10,9},{11,1... | collective-permute-start | bytes 3311624 | tf_op jit(solution)/shard_map/ppermute | solution.py:49
  50.5 16.1 %collective-permute-start.6 = (bf16[4,88,704]{2,1,0:T(8,128)(2,1)S(1)}, bf16[4,88,704]{2,1,0:T(8,128)(2,1)S(1)}, u32[]{:S(2)}, u32[]{:S(2)}) collective-permute-start(bf16[4,88,704]{2,1,0:T(8,128)(2,1)S(1)} %get-tuple-element.39.refs_0_), channel_id=1, source_target_pairs={{128,0},{129,1},{130,2},{131,3},{132,4},{133,5},{134,6},{135,7},{1... | collective-permute-start | bytes 1486856 | tf_op jit(solution)/shard_map/ppermute | solution.py:49
  55.7 17.4 %collective-permute-start.8 = (bf16[4,88,704]{2,1,0:T(8,128)(2,1)S(1)}, bf16[4,88,704]{2,1,0:T(8,128)(2,1)S(1)}, u32[]{:S(2)}, u32[]{:S(2)}) collective-permute-start(bf16[4,88,704]{2,1,0:T(8,128)(2,1)S(1)} %get-tuple-element.39.refs_0_), channel_id=1, source_target_pairs={{384,0},{385,1},{386,2},{387,3},{388,4},{389,5},{390,6},{391,7},{3... | collective-permute-start | bytes 1486856 | tf_op jit(solution)/shard_map/ppermute | solution.py:49
  57.6 26.9 %collective-permute-start.11 = (bf16[4,88,704]{2,1,0:T(8,128)(2,1)S(1)}, bf16[4,88,704]{2,1,0:T(8,128)(2,1)S(1)}, u32[]{:S(2)}, u32[]{:S(2)}) collective-permute-start(bf16[4,88,704]{2,1,0:T(8,128)(2,1)S(1)} %get-tuple-element.48.refs_0_), channel_id=1, source_target_pairs={{384,0},{385,1},{386,2},{387,3},{388,4},{389,5},{390,6},{391,7},{3... | collective-permute-start | bytes 1486856 | tf_op jit(solution)/shard_map/ppermute | solution.py:49
  66.6 28.3 %collective-permute-start.7 = (bf16[4,88,704]{2,1,0:T(8,128)(2,1)S(1)}, bf16[4,88,704]{2,1,0:T(8,128)(2,1)S(1)}, u32[]{:S(2)}, u32[]{:S(2)}) collective-permute-start(bf16[4,88,704]{2,1,0:T(8,128)(2,1)S(1)} %collective-permute-done.6.refs_1_), channel_id=1, source_target_pairs={{128,0},{129,1},{130,2},{131,3},{132,4},{133,5},{134,6},{135,7},{1... | collective-permute-start | bytes 1486856 | tf_op jit(solution)/shard_map/ppermute | solution.py:49
  73.1 26.0 %collective-permute-start.10 = (bf16[4,88,704]{2,1,0:T(8,128)(2,1)S(1)}, bf16[4,88,704]{2,1,0:T(8,128)(2,1)S(1)}, u32[]{:S(2)}, u32[]{:S(2)}) collective-permute-start(bf16[4,88,704]{2,1,0:T(8,128)(2,1)S(1)} %get-tuple-element.48.refs_0_), channel_id=1, source_target_pairs={{128,0},{129,1},{130,2},{131,3},{132,4},{133,5},{134,6},{135,7},{1... | collective-permute-start | bytes 1486856 | tf_op jit(solution)/shard_map/ppermute | solution.py:49
  84.5 16.6 %collective-permute-start.12 = (bf16[4,88,704]{2,1,0:T(8,128)(2,1)S(1)}, bf16[4,88,704]{2,1,0:T(8,128)(2,1)S(1)}, u32[]{:S(2)}, u32[]{:S(2)}) collective-permute-start(bf16[4,88,704]{2,1,0:T(8,128)(2,1)S(1)} %collective-permute-done.11.refs_3_), channel_id=1, source_target_pairs={{384,0},{385,1},{386,2},{387,3},{388,4},{389,5},{390,6},{391,7},{3... | collective-permute-start | bytes 1486856 | tf_op jit(solution)/shard_map/ppermute | solution.py:49
  95.0 9.5 %copy-start.5 = (f32[2816]{0:T(1024)S(1)}, f32[2816]{0:T(1024)}, u32[]{:S(2)}) copy-start(f32[2816]{0:T(1024)} %refs_7_.1) | copy-start | bytes 33796
  95.1 9.5 %copy-start.8 = (f32[704]{0:T(1024)S(1)}, f32[704]{0:T(1024)}, u32[]{:S(2)}) copy-start(f32[704]{0:T(1024)} %refs_5_.1) | copy-start | bytes 8452
  95.1 9.5 %copy-start.9 = (f32[704]{0:T(1024)S(1)}, f32[704]{0:T(1024)}, u32[]{:S(2)}) copy-start(f32[704]{0:T(1024)} %refs_6_.1) | copy-start | bytes 8452
  95.1 9.5 %collective-permute-start.9 = (bf16[4,4,88,704]{3,2,1,0:T(8,128)(2,1)S(1)}, bf16[4,4,88,704]{3,2,1,0:T(8,128)(2,1)S(1)}, u32[]{:S(2)}, u32[]{:S(2)}) collective-permute-start(bf16[4,4,88,704]{3,2,1,0:T(8,128)(2,1)S(1)} %join.2.refs_8_), channel_id=1, source_target_pairs={{32,0},{33,1},{34,2},{35,3},{36,4},{37,5},{38,6},{39,7},{40,8},{41... | collective-permute-start | bytes 5947400 | tf_op jit(solution)/shard_map/ppermute | solution.py:49
  101.2 12.5 %copy-start.6 = (f32[2816]{0:T(1024)S(1)}, f32[2816]{0:T(1024)}, u32[]{:S(2)}) copy-start(f32[2816]{0:T(1024)} %gamma_ref.1) | copy-start | bytes 33796
  101.3 12.5 %copy-start.7 = (f32[2816]{0:T(1024)S(1)}, f32[2816]{0:T(1024)}, u32[]{:S(2)}) copy-start(f32[2816]{0:T(1024)} %beta_ref.1) | copy-start | bytes 33796
  101.3 12.5 %copy-start.10 = (f32[704]{0:T(1024)S(1)}, f32[704]{0:T(1024)}, u32[]{:S(2)}) copy-start(f32[704]{0:T(1024)} %dbias_ref.1) | copy-start | bytes 8452
  101.3 12.5 %collective-permute-start.13 = (bf16[4,4,88,704]{3,2,1,0:T(8,128)(2,1)S(1)}, bf16[4,4,88,704]{3,2,1,0:T(8,128)(2,1)S(1)}, u32[]{:S(2)}, u32[]{:S(2)}) collective-permute-start(bf16[4,4,88,704]{3,2,1,0:T(8,128)(2,1)S(1)} %join.3.refs_0_), channel_id=1, source_target_pairs={{32,0},{33,1},{34,2},{35,3},{36,4},{37,5},{38,6},{39,7},{40,8},{41... | collective-permute-start | bytes 5947400 | tf_op jit(solution)/shard_map/ppermute | solution.py:49

commit v3 on v2

--- a/solution.py
+++ b/solution.py
@@ -1,3 +1,5 @@
+import functools
+
 import jax
 import jax.numpy as jnp
 from jax import lax
@@ -9,6 +11,9 @@
 PIX = H * W
 LANES = 128
 CHUNKS = 6
+LOW = 400
+TAIL = C - (CHUNKS - 1) * LANES
+SENT = (CHUNKS - 1) * PIX + LOW
 SHARD = 88
 MIB = 1024 * 1024
 OFFSETS = ((0, 1, 7, 2), (4, 5, 3, 6))
@@ -68,26 +73,55 @@
     return jnp.concatenate([value, zeros], axis=-1)
 
 
+def sent_chunk(ref, n, first, offset, count):
+    if n < CHUNKS - 1:
+        return ref[pl.ds(pl.multiple_of(n * PIX + first + offset, 16), count), :].astype(jnp.float32)
+    rows = pl.ds(pl.multiple_of(n * PIX + offset, 16), count)
+    part = slice(0, TAIL) if first < LOW else slice(TAIL, LANES)
+    return widen(ref[rows, part].astype(jnp.float32))
+
+
 def lanes(chunk):
     return slice(chunk * LANES, min((chunk + 1) * LANES, C))
 
 
-def flatten_kernel(clip_ref, x_ref, flat_ref, masked_ref):
+def flatten_kernel(clip_ref, x_ref, flat_ref, plain_ref, masked_ref):
     keep = (1 - clip_ref[0]).astype(jnp.float32)
+
+    def put(first, rows):
+        count = rows.shape[0]
+        for n in range(CHUNKS):
+            part, start = slice(0, LANES), n * PIX + first
+            if n == CHUNKS - 1:
+                part = slice(0, TAIL) if first < LOW else slice(TAIL, LANES)
+                start = start if first < LOW else start - LOW
+            value = rows[:, lanes(n)]
+            plain_ref[start : start + count, part] = value.astype(jnp.bfloat16)
+            masked_ref[start : start + count, part] = (value * keep).astype(jnp.bfloat16)
+
     for g in range(7):
         rows = jnp.concatenate([x_ref[4 * g + r].astype(jnp.float32) for r in range(4)], axis=0)
         flat_ref[112 * g : 112 * (g + 1), :] = rows.astype(jnp.bfloat16)
-        masked_ref[112 * g : 112 * (g + 1), :] = (rows * keep).astype(jnp.bfloat16)
+        cut = LOW - 112 * g
+        if 0 < cut < 112:
+            put(112 * g, rows[:cut])
+            put(LOW, rows[cut:])
+        else:
+            put(112 * g, rows)
+    blank = jnp.zeros((2 * LOW - PIX, LANES - TAIL), jnp.bfloat16)
+    plain_ref[SENT - (2 * LOW - PIX) :, TAIL:] = blank
+    masked_ref[SENT - (2 * LOW - PIX) :, TAIL:] = blank
 
 
 def flatten(clip, frame):
-    out = jax.ShapeDtypeStruct((PIX, C), jnp.bfloat16)
+    flat_shape = jax.ShapeDtypeStruct((PIX, C), jnp.bfloat16)
+    packed = jax.ShapeDtypeStruct((SENT, LANES), jnp.bfloat16)
     return pl.pallas_call(
         flatten_kernel,
-        out_shape=(out, out),
+        out_shape=(flat_shape, packed, packed),
         in_specs=[smem_spec, vmem_spec],
-        out_specs=(vmem_spec, vmem_spec),
-        compiler_params=pltpu.CompilerParams(vmem_limit_bytes=8 * MIB),
+        out_specs=(vmem_spec, vmem_spec, vmem_spec),
+        compiler_params=pltpu.CompilerParams(vmem_limit_bytes=12 * MIB),
         name="flatten",
     )(clip, frame)
 
@@ -197,14 +231,14 @@
     gain = [widen(gain_ref[lanes(n)][None]) for n in range(CHUNKS)]
     nbias = [widen(nbias_ref[lanes(n)][None]) for n in range(CHUNKS)]
 
-    def norm_rows(step, carry):
-        rows = pl.ds(pl.multiple_of(step * 112, 16), 112)
+    def norm_rows(first, count, step, carry):
+        rows = pl.ds(pl.multiple_of(first + step * count, 16), count)
         parts = []
         for n in range(CHUNKS):
             part = lanes(n)
             base = c0_ref[n, rows, :] if n < 3 else c1_ref[n - 3, rows, :]
-            before = widen(prev_ref[rows, part].astype(jnp.float32)) * (widen(t_ref[0:1, part]) * keep)
-            after = widen(next_ref[rows, part].astype(jnp.float32)) * widen(t_ref[2:3, part])
+            before = sent_chunk(prev_ref, n, first, step * count, count) * (widen(t_ref[0:1, part]) * keep)
+            after = sent_chunk(next_ref, n, first, step * count, count) * widen(t_ref[2:3, part])
             parts.append(base + before + after)
         total = parts[0]
         for n in range(1, CHUNKS):
@@ -223,7 +257,8 @@
             normed[rows, n * LANES : (n + 1) * LANES] = value.astype(jnp.bfloat16)
         return carry
 
-    lax.fori_loop(0, PIX // 112, norm_rows, 0)
+    lax.fori_loop(0, 5, functools.partial(norm_rows, 0, 80), 0)
+    lax.fori_loop(0, 4, functools.partial(norm_rows, LOW, 96), 0)
 
     def units(step, carry):
         cols = pl.ds(pl.multiple_of(step * 256, 256), 256)
@@ -337,9 +372,9 @@
     both = jnp.stack([up_weight.T, down_weight])
     blocks = spread_yz(both)
     conv0 = conv(0, 3, frame, space_kernel, time_kernel, conv_bias)
-    flat_frame, masked = flatten(clip_cut, frame)
+    flat_frame, plain, masked = flatten(clip_cut, frame)
     blocks = [after(block, flat_frame, conv0) for block in blocks]
-    prev = permute(after(flat_frame, *blocks), from_frame(-1))
+    prev = permute(after(plain, *blocks), from_frame(-1))
     nxt = permute(after(masked, *blocks), from_frame(1))
     up_yz, down_yz = split(blocks)
     conv1 = conv(3, 3, frame, space_kernel, time_kernel, after(conv_bias, up_yz))
@@ -349,9 +384,9 @@
     down_1 = from_x(after(down_yz, conv1, up_1), 1)
     up_2 = from_x(after(up_1, conv1), 1)
     down_2 = from_x(after(down_3, up_3), 3)
-    up_own = join([after(block, prev) for block in (up_yz, up_1, up_2, up_3)])
+    up_own = join([up_yz, up_1, up_2, up_3])
     up_other = swap_core(up_own)
-    down_own = join([after(block, nxt) for block in (down_yz, down_1, down_2, down_3)])
+    down_own = join([after(block, prev, nxt) for block in (down_yz, down_1, down_2, down_3)])
     down_other = swap_core(down_own)
     hid, energy = up(
         clip_cut,

time: 121 us -> 122 us (level)
  waiting for transfers between devices: 30.7 us -> 32.3 us
  starting transfers between devices: 54.8 us -> 53.3 us
    ppermute x14, waiting for transfers between devices: 30.7 us -> 32.3 us  [permute(): return lax.ppermute(value, ('video', 'tm'), pairs)]
    ppermute x14, starting transfers between devices: 54.8 us -> 53.3 us  [permute(): return lax.ppermute(value, ('video', 'tm'), pairs)]
  transfers between devices with their start and end apart: 14 -> 14, of which waited for: 6 -> 8; matrix products, arithmetic and copies ran while one was open for 0% -> 0% of each run, Pallas kernels for 20% -> 20%
where the time goes in v3:
time: 122 us; the launch traced here: 121 us
  starting transfers between devices  53.3 us (44%)
  waiting for transfers between devices  32.3 us (26%)
  Pallas kernels  31.6 us (26%)
  local copies, waits for them, and re-layouts  2.28 us (2%)
    ppermute x14, starting transfers between devices, permute(): return lax.ppermute(value, ('video', 'tm'), pairs)  53.3 us
    ppermute x14, waiting for transfers between devices, permute(): return lax.ppermute(value, ('video', 'tm'), pairs)  32.3 us
    pallas_call x2, Pallas kernels, conv(): pl.pallas_call(lambda *refs: conv_kernel(first, count, *refs), out_shape=...  14.1 us
    pallas_call x1, Pallas kernels, up(): pl.pallas_call(up_kernel, out_shape=(jax.ShapeDtypeStruct((PIX, HID), jnp...  9.74 us
    pallas_call x1, Pallas kernels, down(): pl.pallas_call(down_kernel, out_shape=jax.ShapeDtypeStruct((H, W, C), jnp...  7.07 us
  transfers between devices with their start and end apart: 14, of which 8 were waited for; matrix products, arithmetic and copies ran while one was open for 0% of the time, Pallas kernels for 20%

profile of v3, /device:TPU:9, one launch (start us, length us, event | category | flops | bytes accessed | tf_op | source)
XLA Modules:
  0.0 121.5 jit_solution(15255451162815141783)
XLA Ops:
  0.0 1.0 pad_maximum_fusion
  1.1 6.6 %collective-permute-start = (bf16[2,88,704]{2,1,0:T(8,128)(2,1)S(1)}, bf16[2,88,704]{2,1,0:T(8,128)(2,1)S(1)}, u32[]{:S(2)}, u32[]{:S(2)}) collective-permute-start(bf16[2,88,704]{2,1,0:T(8,128)(2,1)S(1)} %pad_maximum_fusion), channel_id=1, source_target_pairs={{0,0},{1,1},{2,2},{3,3},{4,4},{5,5},{6,6},{7,7},{8,8},{9,9},{10,10... | collective-permute-start | bytes 743432 | tf_op jit(solution)/shard_map/ppermute | solution.py:54
  7.6 3.6 %collective-permute-start.1 = (bf16[2,88,704]{2,1,0:T(8,128)(2,1)S(1)}, bf16[2,88,704]{2,1,0:T(8,128)(2,1)S(1)}, u32[]{:S(2)}, u32[]{:S(2)}) collective-permute-start(bf16[2,88,704]{2,1,0:T(8,128)(2,1)S(1)} %pad_maximum_fusion), channel_id=1, source_target_pairs={{5,0},{4,1},{7,2},{6,3},{9,4},{8,5},{11,6},{10,7},{13,8},{12,9},{1... | collective-permute-start | bytes 743432 | tf_op jit(solution)/shard_map/ppermute | solution.py:54
  11.2 10.1 %collective-permute-start.2 = (bf16[2,88,704]{2,1,0:T(8,128)(2,1)S(1)}, bf16[2,88,704]{2,1,0:T(8,128)(2,1)S(1)}, u32[]{:S(2)}, u32[]{:S(2)}) collective-permute-start(bf16[2,88,704]{2,1,0:T(8,128)(2,1)S(1)} %pad_maximum_fusion), channel_id=1, source_target_pairs={{30,0},{31,1},{28,2},{29,3},{2,4},{3,5},{0,6},{1,7},{6,8},{7,9},{4... | collective-permute-start | bytes 743432 | tf_op jit(solution)/shard_map/ppermute | solution.py:54
  21.3 1.9 %collective-permute-start.3 = (bf16[2,88,704]{2,1,0:T(8,128)(2,1)S(1)}, bf16[2,88,704]{2,1,0:T(8,128)(2,1)S(1)}, u32[]{:S(2)}, u32[]{:S(2)}) collective-permute-start(bf16[2,88,704]{2,1,0:T(8,128)(2,1)S(1)} %pad_maximum_fusion), channel_id=1, source_target_pairs={{11,0},{10,1},{9,2},{8,3},{15,4},{14,5},{13,6},{12,7},{19,8},{18,9... | collective-permute-start | bytes 743432 | tf_op jit(solution)/shard_map/ppermute | solution.py:54
  23.9 0.0 copy-start
  23.9 1.3 %copy-done = bf16[1,28,28,704]{3,2,1,0:T(8,128)(2,1)S(1)} copy-done((bf16[1,28,28,704]{3,2,1,0:T(8,128)(2,1)S(1)}, bf16[1,28,28,704]{3,2,1,0:T(8,128)(2,1)}, u32[]{:S(2)}) %copy-start) | copy-done | bytes 1103896
  25.3 0.4 flatten.1
  25.7 0.9 copy-done.1
  26.6 7.0 %conv.2.refs_0_ = f32[3,784,128]{2,1,0:T(8,128)S(1)} custom-call(bf16[28,28,704]{2,1,0:T(8,128)(2,1)S(1)} %bitcast.7, f32[49,704]{1,0:T(8,128)S(1)} %copy-done.2, f32[3,704]{1,0:T(4,128)S(1)} %copy-done.3, f32[704]{0:T(1024)S(1)} %copy-done.4), custom_call_target="tpu_custom_call" | custom-call | tf_op jit(solution)/shard_map/conv/pallas_call | solution.py:164
  33.6 0.0 collective-permute-done.refs_0_
  33.6 0.0 collective-permute-done.1.refs_1_
  33.6 0.3 collective-permute-done.2.refs_2_
  33.9 8.6 %collective-permute-done.3.refs_3_ = bf16[2,88,704]{2,1,0:T(8,128)(2,1)S(1)} collective-permute-done((bf16[2,88,704]{2,1,0:T(8,128)(2,1)S(1)}, bf16[2,88,704]{2,1,0:T(8,128)(2,1)S(1)}, u32[]{:S(2)}, u32[]{:S(2)}) %collective-permute-start.3) | collective-permute-done | bytes 247840 | tf_op jit(solution)/shard_map/ppermute | solution.py:54
  42.5 1.9 %collective-permute-start.4 = (bf16[4320,128]{1,0:T(8,128)(2,1)S(1)}, bf16[4320,128]{1,0:T(8,128)(2,1)S(1)}, u32[]{:S(2)}, u32[]{:S(2)}) collective-permute-start(bf16[4320,128]{1,0:T(8,128)(2,1)S(1)} %get-tuple-element.34), channel_id=1, source_target_pairs={{0,1},{1,2},{2,3},{3,4},{4,5},{5,6},{6,7},{7,8},{8,9},{9,10},{10,1... | collective-permute-start | bytes 3317768 | tf_op jit(solution)/shard_map/ppermute | solution.py:54
  44.4 6.1 %collective-permute-start.5 = (bf16[4320,128]{1,0:T(8,128)(2,1)S(1)}, bf16[4320,128]{1,0:T(8,128)(2,1)S(1)}, u32[]{:S(2)}, u32[]{:S(2)}) collective-permute-start(bf16[4320,128]{1,0:T(8,128)(2,1)S(1)} %get-tuple-element.36), channel_id=1, source_target_pairs={{1,0},{2,1},{3,2},{4,3},{5,4},{6,5},{7,6},{8,7},{9,8},{10,9},{11,1... | collective-permute-start | bytes 3317768 | tf_op jit(solution)/shard_map/ppermute | solution.py:54
  50.4 0.1 split.1
  50.5 5.2 %collective-permute-start.6 = (bf16[4,88,704]{2,1,0:T(8,128)(2,1)S(1)}, bf16[4,88,704]{2,1,0:T(8,128)(2,1)S(1)}, u32[]{:S(2)}, u32[]{:S(2)}) collective-permute-start(bf16[4,88,704]{2,1,0:T(8,128)(2,1)S(1)} %get-tuple-element.31.refs_0_), channel_id=1, source_target_pairs={{128,0},{129,1},{130,2},{131,3},{132,4},{133,5},{134,6},{135,7},{1... | collective-permute-start | bytes 1486856 | tf_op jit(solution)/shard_map/ppermute | solution.py:54
  55.7 1.9 %collective-permute-start.8 = (bf16[4,88,704]{2,1,0:T(8,128)(2,1)S(1)}, bf16[4,88,704]{2,1,0:T(8,128)(2,1)S(1)}, u32[]{:S(2)}, u32[]{:S(2)}) collective-permute-start(bf16[4,88,704]{2,1,0:T(8,128)(2,1)S(1)} %get-tuple-element.31.refs_0_), channel_id=1, source_target_pairs={{384,0},{385,1},{386,2},{387,3},{388,4},{389,5},{390,6},{391,7},{3... | collective-permute-start | bytes 1486856 | tf_op jit(solution)/shard_map/ppermute | solution.py:54
  57.6 1.9 %collective-permute-start.11 = (bf16[4,88,704]{2,1,0:T(8,128)(2,1)S(1)}, bf16[4,88,704]{2,1,0:T(8,128)(2,1)S(1)}, u32[]{:S(2)}, u32[]{:S(2)}) collective-permute-start(bf16[4,88,704]{2,1,0:T(8,128)(2,1)S(1)} %get-tuple-element.42.refs_0_), channel_id=1, source_target_pairs={{384,0},{385,1},{386,2},{387,3},{388,4},{389,5},{390,6},{391,7},{3... | collective-permute-start | bytes 1486856 | tf_op jit(solution)/shard_map/ppermute | solution.py:54
  59.6 7.0 %conv.3.refs_1_ = f32[3,784,128]{2,1,0:T(8,128)S(1)} custom-call(bf16[28,28,704]{2,1,0:T(8,128)(2,1)S(1)} %bitcast.8, f32[49,704]{1,0:T(8,128)S(1)} %copy-done.2, f32[3,704]{1,0:T(4,128)S(1)} %copy-done.3, f32[704]{0:T(1024)S(1)} %copy-done.4), custom_call_target="tpu_custom_call" | custom-call | tf_op jit(solution)/shard_map/conv/pallas_call | solution.py:164
  66.6 0.0 collective-permute-done.6.refs_1_
  66.6 4.6 %collective-permute-start.7 = (bf16[4,88,704]{2,1,0:T(8,128)(2,1)S(1)}, bf16[4,88,704]{2,1,0:T(8,128)(2,1)S(1)}, u32[]{:S(2)}, u32[]{:S(2)}) collective-permute-start(bf16[4,88,704]{2,1,0:T(8,128)(2,1)S(1)} %collective-permute-done.6.refs_1_), channel_id=1, source_target_pairs={{128,0},{129,1},{130,2},{131,3},{132,4},{133,5},{134,6},{135,7},{1... | collective-permute-start | bytes 1486856 | tf_op jit(solution)/shard_map/ppermute | solution.py:54
  71.2 1.9 %collective-permute-done.8.refs_3_ = bf16[4,88,704]{2,1,0:T(8,128)(2,1)S(1)} collective-permute-done((bf16[4,88,704]{2,1,0:T(8,128)(2,1)S(1)}, bf16[4,88,704]{2,1,0:T(8,128)(2,1)S(1)}, u32[]{:S(2)}, u32[]{:S(2)}) %collective-permute-start.8) | collective-permute-done | bytes 495648 | tf_op jit(solution)/shard_map/ppermute | solution.py:54
  73.1 1.9 %collective-permute-start.10 = (bf16[4,88,704]{2,1,0:T(8,128)(2,1)S(1)}, bf16[4,88,704]{2,1,0:T(8,128)(2,1)S(1)}, u32[]{:S(2)}, u32[]{:S(2)}) collective-permute-start(bf16[4,88,704]{2,1,0:T(8,128)(2,1)S(1)} %get-tuple-element.42.refs_0_), channel_id=1, source_target_pairs={{128,0},{129,1},{130,2},{131,3},{132,4},{133,5},{134,6},{135,7},{1... | collective-permute-start | bytes 1486856 | tf_op jit(solution)/shard_map/ppermute | solution.py:54
  75.0 9.5 %collective-permute-done.11.refs_3_ = bf16[4,88,704]{2,1,0:T(8,128)(2,1)S(1)} collective-permute-done((bf16[4,88,704]{2,1,0:T(8,128)(2,1)S(1)}, bf16[4,88,704]{2,1,0:T(8,128)(2,1)S(1)}, u32[]{:S(2)}, u32[]{:S(2)}) %collective-permute-start.11) | collective-permute-done | bytes 495648 | tf_op jit(solution)/shard_map/ppermute | solution.py:54
  84.5 1.9 %collective-permute-start.12 = (bf16[4,88,704]{2,1,0:T(8,128)(2,1)S(1)}, bf16[4,88,704]{2,1,0:T(8,128)(2,1)S(1)}, u32[]{:S(2)}, u32[]{:S(2)}) collective-permute-start(bf16[4,88,704]{2,1,0:T(8,128)(2,1)S(1)} %collective-permute-done.11.refs_3_), channel_id=1, source_target_pairs={{384,0},{385,1},{386,2},{387,3},{388,4},{389,5},{390,6},{391,7},{3... | collective-permute-start | bytes 1486856 | tf_op jit(solution)/shard_map/ppermute | solution.py:54
  86.5 0.0 collective-permute-done.7.refs_2_
  86.5 0.1 join.2.refs_8_
  86.6 0.0 copy-start.5
  86.6 0.0 copy-start.8
  86.6 0.0 copy-start.9
  86.7 2.4 %collective-permute-start.9 = (bf16[4,4,88,704]{3,2,1,0:T(8,128)(2,1)S(1)}, bf16[4,4,88,704]{3,2,1,0:T(8,128)(2,1)S(1)}, u32[]{:S(2)}, u32[]{:S(2)}) collective-permute-start(bf16[4,4,88,704]{3,2,1,0:T(8,128)(2,1)S(1)} %join.2.refs_8_), channel_id=1, source_target_pairs={{32,0},{33,1},{34,2},{35,3},{36,4},{37,5},{38,6},{39,7},{40,8},{41... | collective-permute-start | bytes 5947400 | tf_op jit(solution)/shard_map/ppermute | solution.py:54
  89.1 1.6 %collective-permute-done.4.refs_2_ = bf16[4320,128]{1,0:T(8,128)(2,1)S(1)} collective-permute-done((bf16[4320,128]{1,0:T(8,128)(2,1)S(1)}, bf16[4320,128]{1,0:T(8,128)(2,1)S(1)}, u32[]{:S(2)}, u32[]{:S(2)}) %collective-permute-start.4) | collective-permute-done | bytes 1105952 | tf_op jit(solution)/shard_map/ppermute | solution.py:54
  90.7 2.8 %collective-permute-done.5.refs_3_ = bf16[4320,128]{1,0:T(8,128)(2,1)S(1)} collective-permute-done((bf16[4320,128]{1,0:T(8,128)(2,1)S(1)}, bf16[4320,128]{1,0:T(8,128)(2,1)S(1)}, u32[]{:S(2)}, u32[]{:S(2)}) %collective-permute-start.5) | collective-permute-done | bytes 1105952 | tf_op jit(solution)/shard_map/ppermute | solution.py:54
  93.5 1.2 collective-permute-done.10.refs_1_
  94.6 6.5 %collective-permute-done.12.refs_2_ = bf16[4,88,704]{2,1,0:T(8,128)(2,1)S(1)} collective-permute-done((bf16[4,88,704]{2,1,0:T(8,128)(2,1)S(1)}, bf16[4,88,704]{2,1,0:T(8,128)(2,1)S(1)}, u32[]{:S(2)}, u32[]{:S(2)}) %collective-permute-start.12) | collective-permute-done | bytes 495648 | tf_op jit(solution)/shard_map/ppermute | solution.py:54
  101.1 0.1 join.3.refs_0_
  101.2 0.0 copy-start.6
  101.3 0.0 copy-start.7
  101.3 0.0 copy-start.10
  101.3 3.3 %collective-permute-start.13 = (bf16[4,4,88,704]{3,2,1,0:T(8,128)(2,1)S(1)}, bf16[4,4,88,704]{3,2,1,0:T(8,128)(2,1)S(1)}, u32[]{:S(2)}, u32[]{:S(2)}) collective-permute-start(bf16[4,4,88,704]{3,2,1,0:T(8,128)(2,1)S(1)} %join.3.refs_0_), channel_id=1, source_target_pairs={{32,0},{33,1},{34,2},{35,3},{36,4},{37,5},{38,6},{39,7},{40,8},{41... | collective-permute-start | bytes 5947400 | tf_op jit(solution)/shard_map/ppermute | solution.py:54
  104.6 0.0 collective-permute-done.9.refs_9_
  104.6 0.0 copy-done.5
  104.6 0.0 copy-done.8
  104.6 9.7 %up.1 = (bf16[784,2816]{1,0:T(8,128)(2,1)S(1)}, f32[1,2816]{1,0:T(1,128)S(1)}) custom-call(s32[1]{0:T(128)S(6)} %copy.14.clip_ref, f32[3,784,128]{2,1,0:T(8,128)S(1)} %conv.2.refs_0_, f32[3,784,128]{2,1,0:T(8,128)S(1)} %conv.3.refs_1_, bf16[4320,128]{1,0:T(8,128)(2,1)S(1)} %collective-permute-done.4.refs_2_, ...), custom_call_target="tpu_custom_call" | custom-call | tf_op jit(solution)/shard_map/up/pallas_call | solution.py:280
  114.3 0.0 collective-permute-done.13.refs_1_
  114.4 7.1 %down.1 = bf16[28,28,704]{2,1,0:T(8,128)(2,1)} custom-call(bf16[784,2816]{1,0:T(8,128)(2,1)S(1)} %get-tuple-element.38.hid_ref, f32[1,2816]{1,0:T(1,128)S(1)} %get-tuple-element.39.energy_ref, f32[2816]{0:T(1024)S(1)} %copy-done.6, f32[2816]{0:T(1024)S(1)} %copy-done.7, f32[704]{0:T(1024)S(1)} %copy-done.10, ...), custom_call_target="tpu_custom_call" | custom-call | tf_op jit(solution)/shard_map/down/pallas_call | solution.py:321
  (11 shorter events, 0.0 us)
Async XLA Ops:
  0.0 25.7 %copy-start.2 = (f32[49,704]{1,0:T(8,128)S(1)}, f32[49,704]{1,0:T(8,128)}, u32[]{:S(2)}) copy-start(f32[49,704]{1,0:T(8,128)} %refs_1_.3) | copy-start | bytes 413956
  0.0 25.7 %copy-start.3 = (f32[3,704]{1,0:T(4,128)S(1)}, f32[3,704]{1,0:T(4,128)}, u32[]{:S(2)}) copy-start(f32[3,704]{1,0:T(4,128)} %refs_4_.1) | copy-start | bytes 25348
  0.0 25.7 %copy-start.4 = (f32[704]{0:T(1024)S(1)}, f32[704]{0:T(1024)}, u32[]{:S(2)}) copy-start(f32[704]{0:T(1024)} %refs_3_.2) | copy-start | bytes 8452
  1.1 32.6 %collective-permute-start = (bf16[2,88,704]{2,1,0:T(8,128)(2,1)S(1)}, bf16[2,88,704]{2,1,0:T(8,128)(2,1)S(1)}, u32[]{:S(2)}, u32[]{:S(2)}) collective-permute-start(bf16[2,88,704]{2,1,0:T(8,128)(2,1)S(1)} %pad_maximum_fusion), channel_id=1, source_target_pairs={{0,0},{1,1},{2,2},{3,3},{4,4},{5,5},{6,6},{7,7},{8,8},{9,9},{10,10... | collective-permute-start | bytes 743432 | tf_op jit(solution)/shard_map/ppermute | solution.py:54
  7.6 26.0 %collective-permute-start.1 = (bf16[2,88,704]{2,1,0:T(8,128)(2,1)S(1)}, bf16[2,88,704]{2,1,0:T(8,128)(2,1)S(1)}, u32[]{:S(2)}, u32[]{:S(2)}) collective-permute-start(bf16[2,88,704]{2,1,0:T(8,128)(2,1)S(1)} %pad_maximum_fusion), channel_id=1, source_target_pairs={{5,0},{4,1},{7,2},{6,3},{9,4},{8,5},{11,6},{10,7},{13,8},{12,9},{1... | collective-permute-start | bytes 743432 | tf_op jit(solution)/shard_map/ppermute | solution.py:54
  11.2 22.7 %collective-permute-start.2 = (bf16[2,88,704]{2,1,0:T(8,128)(2,1)S(1)}, bf16[2,88,704]{2,1,0:T(8,128)(2,1)S(1)}, u32[]{:S(2)}, u32[]{:S(2)}) collective-permute-start(bf16[2,88,704]{2,1,0:T(8,128)(2,1)S(1)} %pad_maximum_fusion), channel_id=1, source_target_pairs={{30,0},{31,1},{28,2},{29,3},{2,4},{3,5},{0,6},{1,7},{6,8},{7,9},{4... | collective-permute-start | bytes 743432 | tf_op jit(solution)/shard_map/ppermute | solution.py:54
  21.3 21.1 %collective-permute-start.3 = (bf16[2,88,704]{2,1,0:T(8,128)(2,1)S(1)}, bf16[2,88,704]{2,1,0:T(8,128)(2,1)S(1)}, u32[]{:S(2)}, u32[]{:S(2)}) collective-permute-start(bf16[2,88,704]{2,1,0:T(8,128)(2,1)S(1)} %pad_maximum_fusion), channel_id=1, source_target_pairs={{11,0},{10,1},{9,2},{8,3},{15,4},{14,5},{13,6},{12,7},{19,8},{18,9... | collective-permute-start | bytes 743432 | tf_op jit(solution)/shard_map/ppermute | solution.py:54
  23.9 1.3 %copy-start = (bf16[1,28,28,704]{3,2,1,0:T(8,128)(2,1)S(1)}, bf16[1,28,28,704]{3,2,1,0:T(8,128)(2,1)}, u32[]{:S(2)}) copy-start(bf16[1,28,28,704]{3,2,1,0:T(8,128)(2,1)} %param.13) | copy-start | bytes 3311620
  25.3 1.3 %copy-start.1 = (bf16[1,28,28,704]{3,2,1,0:T(8,128)(2,1)S(1)}, bf16[1,28,28,704]{3,2,1,0:T(8,128)(2,1)}, u32[]{:S(2)}) copy-start(bf16[1,28,28,704]{3,2,1,0:T(8,128)(2,1)} %param.13) | copy-start | bytes 3311620
  42.5 48.2 %collective-permute-start.4 = (bf16[4320,128]{1,0:T(8,128)(2,1)S(1)}, bf16[4320,128]{1,0:T(8,128)(2,1)S(1)}, u32[]{:S(2)}, u32[]{:S(2)}) collective-permute-start(bf16[4320,128]{1,0:T(8,128)(2,1)S(1)} %get-tuple-element.34), channel_id=1, source_target_pairs={{0,1},{1,2},{2,3},{3,4},{4,5},{5,6},{6,7},{7,8},{8,9},{9,10},{10,1... | collective-permute-start | bytes 3317768 | tf_op jit(solution)/shard_map/ppermute | solution.py:54
  44.4 49.1 %collective-permute-start.5 = (bf16[4320,128]{1,0:T(8,128)(2,1)S(1)}, bf16[4320,128]{1,0:T(8,128)(2,1)S(1)}, u32[]{:S(2)}, u32[]{:S(2)}) collective-permute-start(bf16[4320,128]{1,0:T(8,128)(2,1)S(1)} %get-tuple-element.36), channel_id=1, source_target_pairs={{1,0},{2,1},{3,2},{4,3},{5,4},{6,5},{7,6},{8,7},{9,8},{10,9},{11,1... | collective-permute-start | bytes 3317768 | tf_op jit(solution)/shard_map/ppermute | solution.py:54
  50.5 16.1 %collective-permute-start.6 = (bf16[4,88,704]{2,1,0:T(8,128)(2,1)S(1)}, bf16[4,88,704]{2,1,0:T(8,128)(2,1)S(1)}, u32[]{:S(2)}, u32[]{:S(2)}) collective-permute-start(bf16[4,88,704]{2,1,0:T(8,128)(2,1)S(1)} %get-tuple-element.31.refs_0_), channel_id=1, source_target_pairs={{128,0},{129,1},{130,2},{131,3},{132,4},{133,5},{134,6},{135,7},{1... | collective-permute-start | bytes 1486856 | tf_op jit(solution)/shard_map/ppermute | solution.py:54
  55.7 17.4 %collective-permute-start.8 = (bf16[4,88,704]{2,1,0:T(8,128)(2,1)S(1)}, bf16[4,88,704]{2,1,0:T(8,128)(2,1)S(1)}, u32[]{:S(2)}, u32[]{:S(2)}) collective-permute-start(bf16[4,88,704]{2,1,0:T(8,128)(2,1)S(1)} %get-tuple-element.31.refs_0_), channel_id=1, source_target_pairs={{384,0},{385,1},{386,2},{387,3},{388,4},{389,5},{390,6},{391,7},{3... | collective-permute-start | bytes 1486856 | tf_op jit(solution)/shard_map/ppermute | solution.py:54
  57.6 26.9 %collective-permute-start.11 = (bf16[4,88,704]{2,1,0:T(8,128)(2,1)S(1)}, bf16[4,88,704]{2,1,0:T(8,128)(2,1)S(1)}, u32[]{:S(2)}, u32[]{:S(2)}) collective-permute-start(bf16[4,88,704]{2,1,0:T(8,128)(2,1)S(1)} %get-tuple-element.42.refs_0_), channel_id=1, source_target_pairs={{384,0},{385,1},{386,2},{387,3},{388,4},{389,5},{390,6},{391,7},{3... | collective-permute-start | bytes 1486856 | tf_op jit(solution)/shard_map/ppermute | solution.py:54
  66.6 19.9 %collective-permute-start.7 = (bf16[4,88,704]{2,1,0:T(8,128)(2,1)S(1)}, bf16[4,88,704]{2,1,0:T(8,128)(2,1)S(1)}, u32[]{:S(2)}, u32[]{:S(2)}) collective-permute-start(bf16[4,88,704]{2,1,0:T(8,128)(2,1)S(1)} %collective-permute-done.6.refs_1_), channel_id=1, source_target_pairs={{128,0},{129,1},{130,2},{131,3},{132,4},{133,5},{134,6},{135,7},{1... | collective-permute-start | bytes 1486856 | tf_op jit(solution)/shard_map/ppermute | solution.py:54
  73.1 21.5 %collective-permute-start.10 = (bf16[4,88,704]{2,1,0:T(8,128)(2,1)S(1)}, bf16[4,88,704]{2,1,0:T(8,128)(2,1)S(1)}, u32[]{:S(2)}, u32[]{:S(2)}) collective-permute-start(bf16[4,88,704]{2,1,0:T(8,128)(2,1)S(1)} %get-tuple-element.42.refs_0_), channel_id=1, source_target_pairs={{128,0},{129,1},{130,2},{131,3},{132,4},{133,5},{134,6},{135,7},{1... | collective-permute-start | bytes 1486856 | tf_op jit(solution)/shard_map/ppermute | solution.py:54
  84.5 16.6 %collective-permute-start.12 = (bf16[4,88,704]{2,1,0:T(8,128)(2,1)S(1)}, bf16[4,88,704]{2,1,0:T(8,128)(2,1)S(1)}, u32[]{:S(2)}, u32[]{:S(2)}) collective-permute-start(bf16[4,88,704]{2,1,0:T(8,128)(2,1)S(1)} %collective-permute-done.11.refs_3_), channel_id=1, source_target_pairs={{384,0},{385,1},{386,2},{387,3},{388,4},{389,5},{390,6},{391,7},{3... | collective-permute-start | bytes 1486856 | tf_op jit(solution)/shard_map/ppermute | solution.py:54
  86.6 17.9 %copy-start.5 = (f32[2816]{0:T(1024)S(1)}, f32[2816]{0:T(1024)}, u32[]{:S(2)}) copy-start(f32[2816]{0:T(1024)} %refs_7_.1) | copy-start | bytes 33796
  86.6 17.9 %copy-start.8 = (f32[704]{0:T(1024)S(1)}, f32[704]{0:T(1024)}, u32[]{:S(2)}) copy-start(f32[704]{0:T(1024)} %refs_5_.1) | copy-start | bytes 8452
  86.6 17.9 %copy-start.9 = (f32[704]{0:T(1024)S(1)}, f32[704]{0:T(1024)}, u32[]{:S(2)}) copy-start(f32[704]{0:T(1024)} %refs_6_.1) | copy-start | bytes 8452
  86.7 17.9 %collective-permute-start.9 = (bf16[4,4,88,704]{3,2,1,0:T(8,128)(2,1)S(1)}, bf16[4,4,88,704]{3,2,1,0:T(8,128)(2,1)S(1)}, u32[]{:S(2)}, u32[]{:S(2)}) collective-permute-start(bf16[4,4,88,704]{3,2,1,0:T(8,128)(2,1)S(1)} %join.2.refs_8_), channel_id=1, source_target_pairs={{32,0},{33,1},{34,2},{35,3},{36,4},{37,5},{38,6},{39,7},{40,8},{41... | collective-permute-start | bytes 5947400 | tf_op jit(solution)/shard_map/ppermute | solution.py:54
  101.2 13.1 %copy-start.6 = (f32[2816]{0:T(1024)S(1)}, f32[2816]{0:T(1024)}, u32[]{:S(2)}) copy-start(f32[2816]{0:T(1024)} %gamma_ref.1) | copy-start | bytes 33796
  101.3 13.1 %copy-start.7 = (f32[2816]{0:T(1024)S(1)}, f32[2816]{0:T(1024)}, u32[]{:S(2)}) copy-start(f32[2816]{0:T(1024)} %beta_ref.1) | copy-start | bytes 33796
  101.3 13.1 %copy-start.10 = (f32[704]{0:T(1024)S(1)}, f32[704]{0:T(1024)}, u32[]{:S(2)}) copy-start(f32[704]{0:T(1024)} %dbias_ref.1) | copy-start | bytes 8452
  101.3 13.1 %collective-permute-start.13 = (bf16[4,4,88,704]{3,2,1,0:T(8,128)(2,1)S(1)}, bf16[4,4,88,704]{3,2,1,0:T(8,128)(2,1)S(1)}, u32[]{:S(2)}, u32[]{:S(2)}) collective-permute-start(bf16[4,4,88,704]{3,2,1,0:T(8,128)(2,1)S(1)} %join.3.refs_0_), channel_id=1, source_target_pairs={{32,0},{33,1},{34,2},{35,3},{36,4},{37,5},{38,6},{39,7},{40,8},{41... | collective-permute-start | bytes 5947400 | tf_op jit(solution)/shard_map/ppermute | solution.py:54
